TPU v7x, 32 devices: a whole 2x2x4 slice. The times are simulated.
32 devices in a mesh: freq: 4 (over z), chan: 8 (over y, x, core).
Axes of the slice: x: 2, y: 2, z: 4, core: 2. Of those that a mesh axis runs over, the one named last changes fastest.
Arguments:
- raw_strain: bfloat16 [8, 32, 150000], P('chan', 'freq'), may hold values from -6 to 6
- fir_taps: bfloat16 [20], replicated, may hold values from -1.25 to 1.25
- band_bins: int32 [240], replicated, may hold values from 60 to 359, as said below
- live_mask: int32 [8, 32], P('chan', 'freq'), may hold values 0 or 1
Outputs:
- cross_spectra: float32 [240, 2, 256, 256], P('freq', None, 'chan')
Inputs may be any that keep to these rules, and one draw needn't show every extreme that they name: `band_bins`: strictly increasing; the first is 60 and the last is 359.
All inputs are finite; a program needn't handle non-finite values. No bound on the sum of `live_mask` on one device may be relied on, other than what follows from the above.
Results may differ from a plain program's by a relative error of at most 0.0067.
Values may be sent and summed in bfloat16 or wider, within the bound.
No kernel may reach another device: no remote copies, remote signals or barrier semaphores. Data moves between devices by JAX's collectives and lax.ppermute only.
A program may use at most 64 MiB of HBM per device.

v0:
```python
import math

import jax
import jax.numpy as jnp
from jax import lax
from jax.sharding import PartitionSpec as P

WIN = 10
DECIM = 10
NT = 1500


def make_table(band_bins, length):
    times = jnp.arange(length, dtype=jnp.int32)[:, None]
    phase = times * band_bins[None, :] % length
    angle = phase.astype(jnp.float32) * jnp.float32(2.0 * math.pi / length)
    return jnp.concatenate([jnp.cos(angle), -jnp.sin(angle)], axis=1).astype(jnp.bfloat16)


def correlate(rows_spec, cols_spec, windows):
    bins = rows_spec.shape[0]
    height = rows_spec.shape[3]
    width = cols_spec.shape[3]
    real_left = rows_spec.reshape(bins, 2 * windows, height)
    imag_left = jnp.concatenate([rows_spec[:, 1], -rows_spec[:, 0]], axis=1)
    left_both = jnp.stack([real_left, imag_left], axis=1)
    right_side = cols_spec.reshape(bins, 2 * windows, width)
    prod = jnp.einsum("fski,fkj->fsij", left_both, right_side, preferred_element_type=jnp.float32)
    return prod / windows


def decimate(raw_strain, fir_taps, rows, windows, length, factor):
    outputs = length // 10
    span = outputs * factor
    blocks = raw_strain.reshape(rows * windows * 10, span)
    taps_float = fir_taps.astype(jnp.float32)
    tap_count = fir_taps.shape[0]
    sample_idx = jnp.arange(span, dtype=jnp.int32)[:, None]
    out_idx = jnp.arange(outputs, dtype=jnp.int32)[None, :]
    tap_idx = factor * out_idx + factor - 1 - sample_idx
    valid = (tap_idx >= 0) & (tap_idx < tap_count)
    band = jnp.where(valid, taps_float[jnp.clip(tap_idx, 0, tap_count - 1)], 0.0).astype(
        jnp.bfloat16
    )
    current = jnp.dot(blocks, band, preferred_element_type=jnp.float32)
    tail = blocks[:, span - factor :]
    tail_taps = taps_float[2 * factor - 1 - jnp.arange(factor, dtype=jnp.int32)].astype(
        jnp.bfloat16
    )
    carried = jnp.dot(tail, tail_taps[:, None], preferred_element_type=jnp.float32)
    carried = carried.reshape(rows * windows, 10)
    carried = jnp.pad(carried, ((0, 0), (1, 0)))[:, :10]
    current = current.reshape(rows * windows, 10, outputs)
    current = current.at[:, :, 0].add(carried)
    return current.reshape(rows, windows, length).astype(jnp.bfloat16)


def shards(raw_strain, fir_taps, band_bins, live_mask):
    rows = raw_strain.shape[1]
    windows = WIN
    length = NT
    factor = DECIM
    bins = band_bins.shape[0]
    table = make_table(band_bins, length)
    decimated = decimate(raw_strain, fir_taps, rows, windows, length, factor)
    spectrum = jnp.dot(
        decimated.reshape(rows * windows, length), table, preferred_element_type=jnp.float32
    )
    spectrum = spectrum.reshape(rows, windows, 2, bins)
    power = jnp.sum(spectrum * spectrum, axis=(2, 3)) / bins
    scale = lax.rsqrt(power + 1e-06) * live_mask[0].astype(jnp.float32)[:, None]
    whitened = (spectrum * scale[:, :, None, None]).astype(jnp.bfloat16)
    ordered = jnp.transpose(whitened, (3, 2, 1, 0))
    own = lax.all_to_all(ordered, "freq", split_axis=0, concat_axis=3, tiled=True)
    return correlate(own, lax.all_gather(own, "chan", axis=3, tiled=True), windows)


def solution(mesh):
    in_specs = (P("chan", "freq", None), P(), P(), P("chan", "freq"))
    out_specs = P("freq", None, "chan", None)
    return jax.shard_map(shards, mesh=mesh, in_specs=in_specs, out_specs=out_specs, check_vma=False)
```

profile of v0, /device:TPU:0, one launch (start us, length us, event | category | flops | bytes accessed | tf_op | source)
XLA Modules:
  0.0 82.6 jit_solution(9209558224427891211)
XLA Ops:
  0.0 2.1 %fusion.129 = (bf16[1]{0:T(256)(128)(2,1)}, bf16[1]{0:T(256)(128)(2,1)}, bf16[1]{0:T(256)(128)(2,1)}, bf16[1]{0:T(256)(128)(2,1)}, bf16[1]{0:T(256)(128)(2,1)}, ...) fusion(bf16[20]{0:T(256)(128)(2,1)} %param.7), kind=kLoop, calls=%fused_computation.157 | loop fusion | bytes 76 | tf_op jit(solution)/shard_map/gather | solution.py:42
  2.1 1.2 %slice.57 = bf16[1]{0:T(256)(128)(2,1)} slice(bf16[20]{0:T(256)(128)(2,1)} %param.7), slice={[17:18]} | slice | bytes 4 | tf_op jit(solution)/shard_map/gather | solution.py:42
  3.3 4.8 %reshape.254 = bf16[1200000]{0:T(1024)(128)(2,1)S(1)} reshape(bf16[1,8,150000]{2,1,0:T(8,128)(2,1)} %param.6) | data formatting | bytes 4800000
  8.1 5.1 %reshape.153 = bf16[800,1500]{1,0:T(8,128)(2,1)} reshape(bf16[1200000]{0:T(1024)(128)(2,1)S(1)} %reshape.254) | data formatting | bytes 4800000 | tf_op jit(solution)/shard_map/reshape | solution.py:35
  13.3 1.0 %slice.63 = bf16[800,10]{1,0:T(8,128)(2,1)S(1)} slice(bf16[800,1500]{1,0:T(8,128)(2,1)} %reshape.153), slice={[0:800], [1490:1500]} | slice | bytes 32000 | tf_op jit(solution)/shard_map/slice | solution.py:46
  14.3 17.4 %convolution_bitcast_fusion = f32[800,150]{0,1:T(8,128)S(1)} fusion(bf16[800,1500]{1,0:T(8,128)(2,1)} %reshape.153, bf16[]{:T(256)} %bitcast.27, bf16[]{:T(256)} %bitcast.28, bf16[]{:T(256)} %bitcast.29, bf16[]{:T(256)} %bitcast.30, bf16[]{:T(256)} %bitcast.31, bf16[]{:T(256)} %bitcast.33, bf16[]{:T(256)} %bitcast.32, bf16[]{:T(256)} %bitcast.2, ...), kind=kOutput, calls=%fused_computation.64 | convolution fusion | flops 370800000 | bytes 2880640 | tf_op jit(solution)/shard_map/dot_general | solution.py:45
  31.7 0.3 copy.30
  32.1 0.1 copy.52
  32.3 0.2 dot_general.24
  32.6 0.7 gather_fusion
  33.5 0.4 copy.32
  34.0 5.3 %scatter-add.4 = f32[80,10,150]{2,1,0:T(8,128)S(1)} dynamic-update-slice(f32[80,10,150]{2,1,0:T(8,128)S(1)} %reshape.154, f32[80,10,1]{2,1,0:T(8,128)S(1)} %slice_add_fusion, s32[]{:T(128)} %constant.58.clone.1, s32[]{:T(128)} %constant.58.clone.1, s32[]{:T(128)} %constant.58.clone.1) | dynamic-update-slice | bytes 6404 | tf_op jit(solution)/shard_map/scatter-add | solution.py:54
  39.4 0.7 reshape.250
  40.1 6.6 %cosine_convert_fusion = (bf16[1500,240]{0,1:T(8,128)(2,1)S(1)}, bf16[1500,240]{0,1:T(8,128)(2,1)S(1)}) fusion(s32[240]{0:T(256)S(1)} %copy-done.1), kind=kLoop, calls=%fused_computation.59 | loop fusion | flops 4320000 | bytes 1440960 | tf_op jit(solution)/shard_map/convert
  46.8 0.7 multiply_reduce_fusion.1
  47.7 1.3 %copy.33 = bf16[240,2,10,8]{2,1,3,0:T(2,128)(2,1)S(1)} copy(bf16[240,2,10,8]{0,2,1,3:T(8,128)(2,1)S(1)} %fusion.103) | data formatting | bytes 153600 | tf_op jit(solution)/shard_map/convert_element_type | solution.py:72
  49.0 1.6 %reshape.256 = bf16[4,2,4800]{2,1,0:T(2,128)(2,1)S(1)} reshape(bf16[240,8,2,10]{3,2,1,0:T(2,128)(2,1)S(1)} %bitcast.166) | data formatting | bytes 153600
  50.5 11.9 %all_to_all.18 = bf16[4,2,4800]{2,1,0:T(2,128)(2,1)S(1)} all-to-all(bf16[4,2,4800]{2,1,0:T(2,128)(2,1)S(1)} %reshape.256), channel_id=1, replica_groups=mesh['freq'=4,'chan'=8] {'freq'}, dimensions={0} | all-to-all | bytes 153600 | tf_op jit(solution)/shard_map/all_to_all | solution.py:74
  62.4 2.3 %reshape.257 = bf16[240,8,2,10]{3,2,1,0:T(2,128)(2,1)S(1)} reshape(bf16[4,2,4800]{2,1,0:T(2,128)(2,1)S(1)} %all_to_all.18) | data formatting | bytes 153600
  64.8 1.3 %copy.47 = bf16[4,60,2,10,8]{1,0,4,3,2:T(4,128)(2,1)S(1)} copy(bf16[4,60,2,10,8]{3,2,4,1,0:T(2,128)(2,1)S(1)} %bitcast.167) | data formatting | bytes 153600 | tf_op jit(solution)/shard_map/all_to_all | solution.py:74
  66.1 12.1 %all_gather.3 = bf16[60,2,10,256]{0,3,2,1:T(8,128)(2,1)S(1)} all-gather(bf16[60,2,10,32]{0,3,2,1:T(8,128)(2,1)S(1)} %bitcast.168), channel_id=1, replica_groups=mesh['freq'=4,'chan'=8] {'chan'}, dimensions={3}, use_global_device_ids=true | all-gather | bytes 691200 | tf_op jit(solution)/shard_map/all_gather | solution.py:75
  78.3 0.9 %copy.46 = bf16[60,20,256,1]{2,1,3,0:T(8,128)(2,1)S(1)} copy(bf16[60,20,256,1]{0,2,1,3:T(8,128)(2,1)S(1)} %bitcast.165) | data formatting | bytes 1228800 | tf_op jit(solution)/shard_map/reshape | solution.py:27
  79.3 0.6 copy.38
  79.9 2.7 %convolution_multiply_fusion = f32[60,2,32,256]{3,2,1,0:T(8,128)} fusion(bf16[60,2,20,32]{3,2,1,0:T(8,128)(2,1)S(1)} %copy.38, bf16[60,20,256,1]{2,1,3,0:T(8,128)(2,1)S(1)} %copy.46), kind=kOutput, calls=%fused_computation.3 | convolution fusion | flops 40304640 | bytes 4700160 | tf_op jit(solution)/shard_map/fski,fkj->fsij/dot_general | solution.py:28
  (24 shorter events, 1.1 us)
Async XLA Ops:
  32.0 0.7 copy-start
  39.3 0.8 copy-start.1
  39.4 7.3 %copy-start.2 = (s32[1,8]{1,0:T(1,128)S(1)}, s32[1,8]{1,0:T(1,128)}, u32[]{:S(2)}) copy-start(s32[1,8]{1,0:T(1,128)} %param.9) | copy-start | bytes 100
where the time goes:
time: 83.1 us; the launch traced here: 82.6 us
  local copies, waits for them, and re-layouts  30.3 us (36%)
  blocking collectives  24 us (29%)
  matrix products  20.8 us (25%)
  other arithmetic  7.29 us (9%)
    dot_general x1, matrix products, decimate(): current = jnp.dot(blocks, band, preferred_element_type=jnp.float32)  17.4 us
    all_gather x1, blocking collectives, shards(): lax.all_gather(own, 'chan', axis=3, tiled=True)  12.1 us
    all_to_all x1, blocking collectives, shards(): lax.all_to_all(ordered, 'freq', split_axis=0, concat_axis=3, tiled=True)  11.9 us
    unnamed x10, local copies, waits for them, and re-layouts  8.94 us
    another operation x1, other arithmetic  6.55 us
    scatter-add x1, local copies, waits for them, and re-layouts, decimate(): current = current.at[:, :, 0].add(carried)  5.28 us
    reshape x1, local copies, waits for them, and re-layouts, decimate(): blocks = raw_strain.reshape(rows * windows * 10, span)  5.14 us
    gather x2, local copies, waits for them, and re-layouts, decimate(): taps_float[jnp.clip(tap_idx, 0, tap_count - 1)]  3.32 us

commit v1 on v0

v1 whole, which is shorter than its diff:
```python
import functools
import math

import jax
import jax.numpy as jnp
from jax import lax
from jax.experimental import pallas as pl
from jax.experimental.pallas import tpu as pltpu
from jax.sharding import PartitionSpec as P

WIN = 10
DECIM = 10
NT = 1500
LANES = 128
SUB = 8
F32 = jnp.float32
BF16 = jnp.bfloat16


def up(value, unit):
    return -(-value // unit) * unit


def iota(shape, axis):
    return lax.broadcasted_iota(jnp.int32, shape, axis)


def wrap(product, length):
    turns = jnp.floor((product.astype(F32) + 0.5) * F32(1.0 / length)).astype(jnp.int32)
    return product - turns * length


def cos_sin(phase, length):
    four = 4 * phase
    quad = jnp.floor((four.astype(F32) + (0.5 * length + 0.5)) * F32(1.0 / length)).astype(jnp.int32)
    angle = (four - quad * length).astype(F32) * F32(2.0 * math.pi / (4 * length))
    sq = angle * angle
    sin = angle * (1.0 + sq * (F32(-1 / 6) + sq * (F32(1 / 120) + sq * (F32(-1 / 5040) + sq * F32(1 / 362880)))))
    cos = 1.0 + sq * (F32(-0.5) + sq * (F32(1 / 24) + sq * (F32(-1 / 720) + sq * (F32(1 / 40320) + sq * F32(-1 / 3628800)))))
    odd = (quad & 1) == 1
    c0 = jnp.where(odd, sin, cos)
    s0 = jnp.where(odd, cos, sin)
    c = jnp.where(((quad + 1) & 2) == 2, -c0, c0)
    s = jnp.where((quad & 2) == 2, -s0, s0)
    return c, s


def front_kernel(dims, mask_ref, x_hbm, taps_ref, bins_ref, *refs):
    windows, length, factor, groups, per_group, half, rows = dims
    outs = refs[:groups]
    x_ref, band_ref, table_ref, lhs_ref, dec_ref, sem = refs[groups:]
    copy = pltpu.make_async_copy(x_hbm.at[0], x_ref, sem)
    copy.start()
    width = groups * 2 * half
    chunk = factor * LANES
    tiles = factor + 1
    tap_count = taps_ref.shape[1]

    taps = jnp.concatenate([taps_ref[...].astype(F32), jnp.zeros((1, LANES - tap_count), F32)], axis=1)
    taps = jnp.broadcast_to(taps, (SUB, LANES))
    base = factor * iota((SUB, LANES), 1) + (factor - 1 + LANES) - iota((SUB, LANES), 0)
    for row in range(0, tiles * LANES, 2 * SUB):
        pair = []
        for start in (row, row + SUB):
            tap = base - start
            tap = jnp.where((tap >= 0) & (tap < tap_count), tap, LANES - 1)
            pair.append(jnp.take_along_axis(taps, tap, axis=1, mode="promise_in_bounds"))
        band_ref[row : row + 2 * SUB, :] = jnp.concatenate(pair, axis=0).astype(BF16)

    own = lax.axis_index("freq")
    bin_count = bins_ref.shape[1]
    held = up(bin_count, LANES)
    bins = bins_ref[...]
    if held > bin_count:
        bins = jnp.concatenate([bins, jnp.zeros((1, held - bin_count), jnp.int32)], axis=1)
    bins = jnp.broadcast_to(bins, (SUB, held))
    lane = iota((SUB, 2 * half), 1)
    is_imag = lane >= half
    columns = []
    for slot in range(groups):
        first = (own ^ slot) * per_group
        real = pltpu.roll(bins, lax.rem(held - first, held), 1)[:, : 2 * half]
        imag = pltpu.roll(bins, lax.rem(held - first + half, held), 1)[:, : 2 * half]
        columns.append(jnp.where(is_imag, imag, real))
    blocks = up(length, LANES) // LANES
    steps = iota((up(blocks, SUB), 2 * half), 0)
    valid = (lane & (half - 1)) < per_group
    for slot in range(groups):
        bins8 = columns[slot]
        turn_rows = [
            cos_sin(wrap((steps[r : r + SUB] * LANES) * bins8, length), length)
            for r in range(0, steps.shape[0], SUB)
        ]
        for row in range(0, LANES, 2 * SUB):
            here = []
            for start in (row, row + SUB):
                c, s = cos_sin(wrap((iota((SUB, 2 * half), 0) + start) * bins8, length), length)
                here.append((
                    jnp.where(valid, jnp.where(is_imag, -s, c), 0.0),
                    jnp.where(valid, jnp.where(is_imag, -c, -s), 0.0),
                ))
            for block in range(blocks):
                turn_c, turn_s = turn_rows[block // SUB]
                at = block % SUB
                turn_c, turn_s = turn_c[at : at + 1], turn_s[at : at + 1]
                value = [v * turn_c + w * turn_s for v, w in here]
                table_ref[
                    block * LANES + row : block * LANES + row + 2 * SUB,
                    slot * 2 * half : (slot + 1) * 2 * half,
                ] = jnp.concatenate(value, axis=0).astype(BF16)

    copy.wait()
    total = x_ref.shape[1]
    chunks = -(-total // chunk)
    entries = [(q, 0) for q in range(chunks)]
    for w in range(1, windows):
        begin = w * length * factor
        entries.append((begin // chunk, begin))
    zero_tile = jnp.zeros((rows, LANES), F32)
    lane8 = iota((rows, LANES), 1)

    def tile_of(entry, tile):
        q, begin = entry
        start = q * chunk + (tile - 1) * LANES
        if start < 0 or start >= total or start + LANES <= begin:
            return zero_tile
        stop = min(start + LANES, total)
        got = x_ref[:, start:stop].astype(F32)
        if stop - start < LANES:
            got = jnp.concatenate([got, jnp.zeros((rows, LANES - (stop - start)), F32)], axis=1)
        if start < begin:
            got = jnp.where(lane8 >= begin - start, got, 0.0)
        return got

    if len(entries) % 2:
        entries.append((chunks, 0))
    for pair in range(0, len(entries), 2):
        for tile in range(tiles):
            both = [tile_of(entries[pair + e], tile) for e in range(2)]
            lhs_ref[pair * rows : (pair + 2) * rows, tile * LANES : (tile + 1) * LANES] = (
                jnp.concatenate(both, axis=0).astype(BF16)
            )
    dec_ref[...] = jnp.dot(lhs_ref[:, 0 : tiles * LANES], band_ref[...], preferred_element_type=F32)

    def dec(entry):
        return dec_ref[entry * rows : (entry + 1) * rows, :]

    spectrum = None
    for block in range(blocks):
        parts = []
        for w in range(windows):
            first, lead = divmod(w * length, LANES)
            entry = first + block
            low = dec(chunks + w - 1) if (block == 0 and w > 0) else dec(entry)
            if lead:
                low = pltpu.roll(low, LANES - lead, 1)
                if entry + 1 < chunks:
                    high = pltpu.roll(dec(entry + 1), LANES - lead, 1)
                    low = jnp.where(lane8 < LANES - lead, low, high)
            left = length - block * LANES
            if left < LANES:
                low = jnp.where(lane8 < left, low, 0.0)
            parts.append(low)
        lhs = jnp.concatenate(parts, axis=0).astype(BF16)
        lhs_ref[0 : windows * rows, block * LANES : (block + 1) * LANES] = lhs
    spectrum = jnp.dot(
        lhs_ref[0 : windows * rows, 0 : blocks * LANES], table_ref[...], preferred_element_type=F32
    )
    power = jnp.sum(spectrum * spectrum, axis=1, keepdims=True) / bin_count
    row = iota((windows * rows, 1), 0) & (rows - 1)
    live = jnp.zeros((windows * rows, 1), F32)
    for r in range(rows):
        live = jnp.where(row == r, mask_ref[0, r].astype(F32), live)
    scale = lax.rsqrt(power + 1e-06) * live
    for slot in range(groups):
        piece = spectrum[:, slot * 2 * half : (slot + 1) * 2 * half] * scale
        outs[slot][...] = piece.astype(BF16)


def front(raw_strain, fir_taps, band_bins, live_mask, groups):
    rows = raw_strain.shape[1]
    bins = band_bins.shape[0]
    per_group = bins // groups
    half = up(per_group, 64)
    dims = (WIN, NT, DECIM, groups, per_group, half, rows)
    width = groups * 2 * half
    total = raw_strain.shape[2]
    chunks = -(-total // (DECIM * LANES))
    entries = up(chunks + WIN - 1, 2)
    blocks = up(NT, LANES)
    vmem = pl.BlockSpec(memory_space=pltpu.VMEM)
    return pl.pallas_call(
        functools.partial(front_kernel, dims),
        out_shape=[jax.ShapeDtypeStruct((WIN * rows, 2 * half), BF16)] * groups,
        in_specs=[
            pl.BlockSpec(memory_space=pltpu.SMEM),
            pl.BlockSpec(memory_space=pltpu.HBM),
            vmem,
            vmem,
        ],
        out_specs=[vmem] * groups,
        scratch_shapes=[
            pltpu.VMEM((rows, total), BF16),
            pltpu.VMEM(((DECIM + 1) * LANES, LANES), BF16),
            pltpu.VMEM((blocks, width), BF16),
            pltpu.VMEM((entries * rows, max((DECIM + 1) * LANES, blocks)), BF16),
            pltpu.VMEM((entries * rows, LANES), F32),
            pltpu.SemaphoreType.DMA,
        ],
        compiler_params=pltpu.CompilerParams(vmem_limit_bytes=20 << 20),
        name="front",
    )(live_mask, raw_strain, fir_taps[None, :], band_bins[None, :])


def correlate_kernel(dims, step_bins, parts_ref, out_ref, *spec_refs):
    windows, rows, zs, blocks, half = dims
    height = rows * zs
    width = height * blocks
    block = lax.axis_index("chan")
    z_own = lax.axis_index("freq")

    @pl.when(pl.program_id(0) == 0)
    def _():
        lane = iota((height, 2 * half), 1)
        for pair in range(0, windows, 2):
            at = pair * rows
            slabs = ([], [])
            for b in range(blocks):
                for z in range(zs):
                    got = parts_ref[block ^ b, z_own ^ z, at : at + 2 * rows, :].astype(F32)
                    slabs[0].append(got[:rows])
                    slabs[1].append(got[rows:])
            mine = ([], [])
            for z in range(zs):
                got = parts_ref[0, z_own ^ z, at : at + 2 * rows, :].astype(F32)
                mine[0].append(got[:rows])
                mine[1].append(got[rows:])
            for e in range(2):
                own = jnp.concatenate(mine[e], axis=0)
                turned = jnp.where(lane < half, pltpu.roll(own, half, 1), -pltpu.roll(own, half, 1))
                tail = jnp.zeros((up(2 * height, LANES) - 2 * height, 2 * half), F32)
                full = jnp.concatenate(slabs[e] + [own, turned, tail], axis=0)
                start = 2 * half * (pair + e)
                for r in range(0, full.shape[0], LANES):
                    spec_refs[r // LANES][start : start + 2 * half, :] = full[r : r + LANES].T

    first = pl.program_id(0) * step_bins
    for k in range(step_bins):
        got = [ref[pl.ds(first + k, 2 * windows, stride=half), :] for ref in spec_refs]
        got = jnp.concatenate(got, axis=1).astype(BF16)
        prod = lax.dot_general(
            got[:, width : width + 2 * height], got[:, :width],
            (((0,), (0,)), ((), ())), preferred_element_type=F32,
        ) * F32(1.0 / windows)
        out_ref[k, 0] = prod[:height]
        out_ref[k, 1] = prod[height:]


def correlate(parts, per_group, rows):
    blocks, zs, full_rows, lanes = parts.shape
    windows = full_rows // rows
    half = lanes // 2
    height = rows * zs
    width = height * blocks
    step_bins = next(s for s in (10, 6, 5, 4, 3, 2, 1) if per_group % s == 0)
    dims = (windows, rows, zs, blocks, half)
    return pl.pallas_call(
        functools.partial(correlate_kernel, dims, step_bins),
        grid=(per_group // step_bins,),
        out_shape=jax.ShapeDtypeStruct((per_group, 2, height, width), F32),
        in_specs=[pl.BlockSpec(memory_space=pltpu.VMEM)],
        out_specs=pl.BlockSpec((step_bins, 2, height, width), lambda i: (i, 0, 0, 0)),
        scratch_shapes=[pltpu.VMEM((windows * 2 * half, LANES), F32)]
        * ((width + up(2 * height, LANES)) // LANES),
        compiler_params=pltpu.CompilerParams(vmem_limit_bytes=16 << 20),
        name="correlate",
    )(parts)


def shards(groups, blocks, raw_strain, fir_taps, band_bins, live_mask):
    rows = raw_strain.shape[1]
    per_group = band_bins.shape[0] // groups
    pieces = front(raw_strain, fir_taps, band_bins, live_mask, groups)
    got = [pieces[0]]
    for slot in range(groups - 1, 0, -1):
        pairs = [(i, i ^ slot) for i in range(groups)]
        got.insert(1, lax.ppermute(pieces[slot], "freq", pairs))
    parts = jnp.stack(got)[None]
    step = 2
    order = []
    while step < blocks:
        order.append(step)
        step *= 2
    order.append(1)
    slots = [0]
    held = {0: parts}
    for step in order:
        base = jnp.concatenate([held[s] for s in slots], axis=0) if len(slots) > 1 else held[slots[0]]
        moved = lax.ppermute(base, "chan", [(i, i ^ step) for i in range(blocks)])
        for n, s in enumerate(list(slots)):
            held[s ^ step] = moved[n : n + 1]
            slots.append(s ^ step)
    parts = jnp.concatenate([held[s] for s in range(blocks)], axis=0)
    return correlate(parts, per_group, rows)


def solution(mesh):
    in_specs = (P("chan", "freq", None), P(), P(), P("chan", "freq"))
    out_specs = P("freq", None, "chan", None)
    body = functools.partial(shards, mesh.shape["freq"], mesh.shape["chan"])
    return jax.shard_map(body, mesh=mesh, in_specs=in_specs, out_specs=out_specs, check_vma=False)
```

time: 83.1 us -> 35.7 us (0.43)
  local copies, waits for them, and re-layouts: 30.3 us -> 3.77 us
  blocking collectives: 24 us -> 0 us
  matrix products: 20.8 us -> 0 us
  waiting for transfers between devices: 0 us -> 13.9 us
  starting transfers between devices: 0 us -> 8.92 us
  Pallas kernels: 0 us -> 8.72 us
  other arithmetic: 7.29 us -> 0.07 us
    dot_general x3 -> x0, matrix products: 20.8 us -> none  [the longest x1 17.4 us: decimate(): current = jnp.dot(blocks, band, preferred_element_type=jnp.float32)]
    ppermute x0 -> x6, waiting for transfers between devices: none -> 13.9 us  [the longest x3 8.35 us: shards(): moved = lax.ppermute(base, 'chan', [(i, i ^ step) for i in range(blocks)])]
    all_gather x1 -> x0, blocking collectives: 12.1 us -> none  [shards(): lax.all_gather(own, 'chan', axis=3, tiled=True)]
    all_to_all x1 -> x0, blocking collectives: 11.9 us -> none  [shards(): lax.all_to_all(ordered, 'freq', split_axis=0, concat_axis=3, tiled=True)]
    ppermute x0 -> x6, starting transfers between devices: none -> 8.92 us  [the longest x3 5.71 us: shards(): got.insert(1, lax.ppermute(pieces[slot], 'freq', pairs))]
    pallas_call x0 -> x2, Pallas kernels: none -> 8.72 us  [the longest x1 4.45 us: correlate(): pl.pallas_call(functools.partial(correlate_kernel, dims, step_bins), grid...]
    another operation x3 -> x0, other arithmetic: 6.66 us -> none
    reshape x3 -> x0, local copies, waits for them, and re-layouts: 6.15 us -> none  [the longest x1 5.14 us: decimate(): blocks = raw_strain.reshape(rows * windows * 10, span)]
  transfers between devices with their start and end apart: 0 -> 6, of which waited for: 0 -> 5; matrix products, arithmetic and copies ran while one was open for 0% -> 0% of each run, Pallas kernels for 0% -> 0%
where the time goes in v1:
time: 35.7 us; the launch traced here: 35.5 us
  waiting for transfers between devices  13.9 us (39%)
  starting transfers between devices  8.92 us (25%)
  Pallas kernels  8.72 us (24%)
  local copies, waits for them, and re-layouts  3.77 us (11%)
    ppermute x3, waiting for transfers between devices, shards(): moved = lax.ppermute(base, 'chan', [(i, i ^ step) for i in range(blocks)])  8.35 us
    ppermute x3, starting transfers between devices, shards(): got.insert(1, lax.ppermute(pieces[slot], 'freq', pairs))  5.71 us
    ppermute x3, waiting for transfers between devices, shards(): got.insert(1, lax.ppermute(pieces[slot], 'freq', pairs))  5.58 us
    pallas_call x1, Pallas kernels, correlate(): pl.pallas_call(functools.partial(correlate_kernel, dims, step_bins), grid...  4.45 us
    pallas_call x1, Pallas kernels, front(): pl.pallas_call(functools.partial(front_kernel, dims), out_shape=[jax.Shap...  4.27 us
    unnamed x14, local copies, waits for them, and re-layouts  3.76 us
    ppermute x3, starting transfers between devices, shards(): moved = lax.ppermute(base, 'chan', [(i, i ^ step) for i in range(blocks)])  3.21 us
  transfers between devices with their start and end apart: 6, of which 5 were waited for; matrix products, arithmetic and copies ran while one was open for 0% of the time, Pallas kernels for 0%

profile of v1, /device:TPU:0, one launch (start us, length us, event | category | flops | bytes accessed | tf_op | source)
XLA Modules:
  0.0 35.5 jit_solution(11631685495482877470)
XLA Ops:
  0.0 0.0 copy-start
  0.0 1.7 %copy-done = bf16[1,8,150000]{2,1,0:T(8,128)(2,1)S(1)} copy-done((bf16[1,8,150000]{2,1,0:T(8,128)(2,1)S(1)}, bf16[1,8,150000]{2,1,0:T(8,128)(2,1)}, u32[]{:S(2)}) %copy-start) | copy-done | bytes 2400024
  1.7 0.0 copy-start.1
  1.7 0.7 %copy-done.1 = s32[240]{0:T(256)S(1)} copy-done((s32[240]{0:T(256)S(1)}, s32[240]{0:T(256)}, u32[]{:S(2)}) %copy-start.1) | copy-done | bytes 984
  2.4 0.0 copy-start.2
  2.4 0.7 %copy-done.2 = s32[1,8]{1,0:T(1,128)S(1)} copy-done((s32[1,8]{1,0:T(1,128)S(1)}, s32[1,8]{1,0:T(1,128)}, u32[]{:S(2)}) %copy-start.2) | copy-done | bytes 56
  3.0 0.0 copy-start.3
  3.0 0.7 %copy-done.3 = bf16[20]{0:T(256)(128)(2,1)S(1)} copy-done((bf16[20]{0:T(256)(128)(2,1)S(1)}, bf16[20]{0:T(256)(128)(2,1)}, u32[]{:S(2)}) %copy-start.3) | copy-done | bytes 64
  3.7 4.3 %front.1 = (bf16[80,128]{1,0:T(8,128)(2,1)S(1)}, bf16[80,128]{1,0:T(8,128)(2,1)S(1)}, bf16[80,128]{1,0:T(8,128)(2,1)S(1)}, bf16[80,128]{1,0:T(8,128)(2,1)S(1)}) custom-call(s32[1,8]{1,0:T(1,128)S(1)} %copy-done.2, bf16[1,8,150000]{2,1,0:T(8,128)(2,1)S(1)} %copy-done, bf16[1,20]{1,0:T(2,128)(2,1)S(1)} %bitcast.13, s32[1,240]{1,0:T(1,128)S(1)} %bitcast.12), custom_call_target="tpu_custom_call" | custom-call | tf_op jit(solution)/shard_map/front/pallas_call | solution.py:192
  7.9 3.1 %collective-permute-start = (bf16[80,128]{1,0:T(8,128)(2,1)S(1)}, bf16[80,128]{1,0:T(8,128)(2,1)S(1)}, u32[]{:S(2)}, u32[]{:S(2)}) collective-permute-start(bf16[80,128]{1,0:T(8,128)(2,1)S(1)} %get-tuple-element.10), channel_id=1, source_target_pairs={{0,8},{8,0},{16,24},{24,16},{1,9},{9,1},{17,25},{25,17},{2,10},{10... | collective-permute-start | bytes 61448 | tf_op jit(solution)/shard_map/ppermute | solution.py:287
  11.1 2.6 %collective-permute-start.1 = (bf16[80,128]{1,0:T(8,128)(2,1)S(1)}, bf16[80,128]{1,0:T(8,128)(2,1)S(1)}, u32[]{:S(2)}, u32[]{:S(2)}) collective-permute-start(bf16[80,128]{1,0:T(8,128)(2,1)S(1)} %get-tuple-element.11), channel_id=1, source_target_pairs={{0,16},{8,24},{16,0},{24,8},{1,17},{9,25},{17,1},{25,9},{2,18},{10... | collective-permute-start | bytes 61448 | tf_op jit(solution)/shard_map/ppermute | solution.py:287
  13.7 0.0 collective-permute-start.2
  13.7 0.0 collective-permute-done
  13.7 2.3 %collective-permute-done.1 = bf16[80,128]{1,0:T(8,128)(2,1)S(1)} collective-permute-done((bf16[80,128]{1,0:T(8,128)(2,1)S(1)}, bf16[80,128]{1,0:T(8,128)(2,1)S(1)}, u32[]{:S(2)}, u32[]{:S(2)}) %collective-permute-start.1) | collective-permute-done | bytes 20512 | tf_op jit(solution)/shard_map/ppermute | solution.py:287
  16.0 3.3 %collective-permute-done.2 = bf16[80,128]{1,0:T(8,128)(2,1)S(1)} collective-permute-done((bf16[80,128]{1,0:T(8,128)(2,1)S(1)}, bf16[80,128]{1,0:T(8,128)(2,1)S(1)}, u32[]{:S(2)}, u32[]{:S(2)}) %collective-permute-start.2) | collective-permute-done | bytes 20512 | tf_op jit(solution)/shard_map/ppermute | solution.py:287
  19.2 1.6 %collective-permute-start.3 = (bf16[1,4,80,128]{3,2,1,0:T(8,128)(2,1)S(1)}, bf16[1,4,80,128]{3,2,1,0:T(8,128)(2,1)S(1)}, u32[]{:S(2)}, u32[]{:S(2)}) collective-permute-start(bf16[1,4,80,128]{3,2,1,0:T(8,128)(2,1)S(1)} %maximum_bitcast_fusion), channel_id=1, source_target_pairs={{0,2},{1,3},{2,0},{3,1},{4,6},{5,7},{6,4},{7,5},{8,10},{9,11},{10,... | collective-permute-start | bytes 245768 | tf_op jit(solution)/shard_map/ppermute | solution.py:299
  20.8 2.9 %collective-permute-done.3 = bf16[1,4,80,128]{3,2,1,0:T(8,128)(2,1)S(1)} collective-permute-done((bf16[1,4,80,128]{3,2,1,0:T(8,128)(2,1)S(1)}, bf16[1,4,80,128]{3,2,1,0:T(8,128)(2,1)S(1)}, u32[]{:S(2)}, u32[]{:S(2)}) %collective-permute-start.3) | collective-permute-done | bytes 81952 | tf_op jit(solution)/shard_map/ppermute | solution.py:299
  23.8 1.6 %collective-permute-start.4 = (bf16[2,4,80,128]{3,2,1,0:T(8,128)(2,1)S(1)}, bf16[2,4,80,128]{3,2,1,0:T(8,128)(2,1)S(1)}, u32[]{:S(2)}, u32[]{:S(2)}) collective-permute-start(bf16[2,4,80,128]{3,2,1,0:T(8,128)(2,1)S(1)} %pad_maximum_fusion.1), channel_id=1, source_target_pairs={{0,4},{1,5},{2,6},{3,7},{4,0},{5,1},{6,2},{7,3},{8,12},{9,13},{10,... | collective-permute-start | bytes 491528 | tf_op jit(solution)/shard_map/ppermute | solution.py:299
  25.4 3.8 %collective-permute-done.4 = bf16[2,4,80,128]{3,2,1,0:T(8,128)(2,1)S(1)} collective-permute-done((bf16[2,4,80,128]{3,2,1,0:T(8,128)(2,1)S(1)}, bf16[2,4,80,128]{3,2,1,0:T(8,128)(2,1)S(1)}, u32[]{:S(2)}, u32[]{:S(2)}) %collective-permute-start.4) | collective-permute-done | bytes 163872 | tf_op jit(solution)/shard_map/ppermute | solution.py:299
  29.2 0.1 collective-permute-start.5
  29.3 1.6 %collective-permute-done.5 = bf16[4,4,80,128]{3,2,1,0:T(8,128)(2,1)S(1)} collective-permute-done((bf16[4,4,80,128]{3,2,1,0:T(8,128)(2,1)S(1)}, bf16[4,4,80,128]{3,2,1,0:T(8,128)(2,1)S(1)}, u32[]{:S(2)}, u32[]{:S(2)}) %collective-permute-start.5) | collective-permute-done | bytes 327712 | tf_op jit(solution)/shard_map/ppermute | solution.py:299
  31.0 4.5 %correlate.1 = f32[60,2,32,256]{3,2,1,0:T(8,128)} custom-call(bf16[8,4,80,128]{3,2,1,0:T(8,128)(2,1)S(1)} %slice_dynamic-update-slice_fusion.parts_ref), custom_call_target="tpu_custom_call" | custom-call | tf_op jit(solution)/shard_map/correlate/pallas_call | solution.py:267
  (11 shorter events, 0.2 us)
Async XLA Ops:
  0.0 1.7 %copy-start = (bf16[1,8,150000]{2,1,0:T(8,128)(2,1)S(1)}, bf16[1,8,150000]{2,1,0:T(8,128)(2,1)}, u32[]{:S(2)}) copy-start(bf16[1,8,150000]{2,1,0:T(8,128)(2,1)} %x_hbm.1) | copy-start | bytes 7200004
  1.7 0.7 %copy-start.1 = (s32[240]{0:T(256)S(1)}, s32[240]{0:T(256)}, u32[]{:S(2)}) copy-start(s32[240]{0:T(256)} %param.6) | copy-start | bytes 2884
  2.4 0.7 %copy-start.2 = (s32[1,8]{1,0:T(1,128)S(1)}, s32[1,8]{1,0:T(1,128)}, u32[]{:S(2)}) copy-start(s32[1,8]{1,0:T(1,128)} %mask_ref.1) | copy-start | bytes 100
  3.0 0.7 %copy-start.3 = (bf16[20]{0:T(256)(128)(2,1)S(1)}, bf16[20]{0:T(256)(128)(2,1)}, u32[]{:S(2)}) copy-start(bf16[20]{0:T(256)(128)(2,1)} %param.5) | copy-start | bytes 124
  7.9 5.7 %collective-permute-start = (bf16[80,128]{1,0:T(8,128)(2,1)S(1)}, bf16[80,128]{1,0:T(8,128)(2,1)S(1)}, u32[]{:S(2)}, u32[]{:S(2)}) collective-permute-start(bf16[80,128]{1,0:T(8,128)(2,1)S(1)} %get-tuple-element.10), channel_id=1, source_target_pairs={{0,8},{8,0},{16,24},{24,16},{1,9},{9,1},{17,25},{25,17},{2,10},{10... | collective-permute-start | bytes 61448 | tf_op jit(solution)/shard_map/ppermute | solution.py:287
  11.1 4.9 %collective-permute-start.1 = (bf16[80,128]{1,0:T(8,128)(2,1)S(1)}, bf16[80,128]{1,0:T(8,128)(2,1)S(1)}, u32[]{:S(2)}, u32[]{:S(2)}) collective-permute-start(bf16[80,128]{1,0:T(8,128)(2,1)S(1)} %get-tuple-element.11), channel_id=1, source_target_pairs={{0,16},{8,24},{16,0},{24,8},{1,17},{9,25},{17,1},{25,9},{2,18},{10... | collective-permute-start | bytes 61448 | tf_op jit(solution)/shard_map/ppermute | solution.py:287
  13.7 5.6 %collective-permute-start.2 = (bf16[80,128]{1,0:T(8,128)(2,1)S(1)}, bf16[80,128]{1,0:T(8,128)(2,1)S(1)}, u32[]{:S(2)}, u32[]{:S(2)}) collective-permute-start(bf16[80,128]{1,0:T(8,128)(2,1)S(1)} %get-tuple-element.12), channel_id=1, source_target_pairs={{0,24},{8,16},{16,8},{24,0},{1,25},{9,17},{17,9},{25,1},{2,26},{10... | collective-permute-start | bytes 61448 | tf_op jit(solution)/shard_map/ppermute | solution.py:287
  19.2 4.5 %collective-permute-start.3 = (bf16[1,4,80,128]{3,2,1,0:T(8,128)(2,1)S(1)}, bf16[1,4,80,128]{3,2,1,0:T(8,128)(2,1)S(1)}, u32[]{:S(2)}, u32[]{:S(2)}) collective-permute-start(bf16[1,4,80,128]{3,2,1,0:T(8,128)(2,1)S(1)} %maximum_bitcast_fusion), channel_id=1, source_target_pairs={{0,2},{1,3},{2,0},{3,1},{4,6},{5,7},{6,4},{7,5},{8,10},{9,11},{10,... | collective-permute-start | bytes 245768 | tf_op jit(solution)/shard_map/ppermute | solution.py:299
  23.8 5.4 %collective-permute-start.4 = (bf16[2,4,80,128]{3,2,1,0:T(8,128)(2,1)S(1)}, bf16[2,4,80,128]{3,2,1,0:T(8,128)(2,1)S(1)}, u32[]{:S(2)}, u32[]{:S(2)}) collective-permute-start(bf16[2,4,80,128]{3,2,1,0:T(8,128)(2,1)S(1)} %pad_maximum_fusion.1), channel_id=1, source_target_pairs={{0,4},{1,5},{2,6},{3,7},{4,0},{5,1},{6,2},{7,3},{8,12},{9,13},{10,... | collective-permute-start | bytes 491528 | tf_op jit(solution)/shard_map/ppermute | solution.py:299
  29.2 1.7 %collective-permute-start.5 = (bf16[4,4,80,128]{3,2,1,0:T(8,128)(2,1)S(1)}, bf16[4,4,80,128]{3,2,1,0:T(8,128)(2,1)S(1)}, u32[]{:S(2)}, u32[]{:S(2)}) collective-permute-start(bf16[4,4,80,128]{3,2,1,0:T(8,128)(2,1)S(1)} %pad_maximum_fusion), channel_id=1, source_target_pairs={{0,1},{1,0},{2,3},{3,2},{4,5},{5,4},{6,7},{7,6},{8,9},{9,8},{10,11... | collective-permute-start | bytes 983048 | tf_op jit(solution)/shard_map/ppermute | solution.py:299

commit v2 on v1

--- a/solution.py
+++ b/solution.py
@@ -45,12 +45,20 @@
     return c, s
 
 
-def front_kernel(dims, mask_ref, x_hbm, taps_ref, bins_ref, *refs):
+def front_kernel(dims, mask_hbm, x_hbm, taps_hbm, bins_hbm, *refs):
     windows, length, factor, groups, per_group, half, rows = dims
     outs = refs[:groups]
-    x_ref, band_ref, table_ref, lhs_ref, dec_ref, sem = refs[groups:]
-    copy = pltpu.make_async_copy(x_hbm.at[0], x_ref, sem)
+    x_ref, mask_ref, taps_ref, bins_ref, band_ref, table_ref, lhs_ref, dec_ref, sems = refs[groups:]
+    small = [
+        pltpu.make_async_copy(src, dst, sems.at[n])
+        for n, (src, dst) in enumerate(((taps_hbm, taps_ref), (bins_hbm, bins_ref), (mask_hbm, mask_ref)))
+    ]
+    for each in small:
+        each.start()
+    copy = pltpu.make_async_copy(x_hbm.at[0], x_ref, sems.at[3])
     copy.start()
+    for each in small:
+        each.wait()
     width = groups * 2 * half
     chunk = factor * LANES
     tiles = factor + 1
@@ -78,7 +86,7 @@
     is_imag = lane >= half
     columns = []
     for slot in range(groups):
-        first = (own ^ slot) * per_group
+        first = lax.rem(own + slot, groups) * per_group
         real = pltpu.roll(bins, lax.rem(held - first, held), 1)[:, : 2 * half]
         imag = pltpu.roll(bins, lax.rem(held - first + half, held), 1)[:, : 2 * half]
         columns.append(jnp.where(is_imag, imag, real))
@@ -192,89 +200,137 @@
     return pl.pallas_call(
         functools.partial(front_kernel, dims),
         out_shape=[jax.ShapeDtypeStruct((WIN * rows, 2 * half), BF16)] * groups,
-        in_specs=[
-            pl.BlockSpec(memory_space=pltpu.SMEM),
-            pl.BlockSpec(memory_space=pltpu.HBM),
-            vmem,
-            vmem,
-        ],
+        in_specs=[pl.BlockSpec(memory_space=pltpu.HBM)] * 4,
         out_specs=[vmem] * groups,
         scratch_shapes=[
             pltpu.VMEM((rows, total), BF16),
+            pltpu.SMEM(live_mask.shape, jnp.int32),
+            pltpu.VMEM((1, fir_taps.shape[0]), BF16),
+            pltpu.VMEM((1, bins), jnp.int32),
             pltpu.VMEM(((DECIM + 1) * LANES, LANES), BF16),
             pltpu.VMEM((blocks, width), BF16),
             pltpu.VMEM((entries * rows, max((DECIM + 1) * LANES, blocks)), BF16),
             pltpu.VMEM((entries * rows, LANES), F32),
-            pltpu.SemaphoreType.DMA,
+            pltpu.SemaphoreType.DMA((4,)),
         ],
         compiler_params=pltpu.CompilerParams(vmem_limit_bytes=20 << 20),
         name="front",
-    )(live_mask, raw_strain, fir_taps[None, :], band_bins[None, :])
-
-
-def correlate_kernel(dims, step_bins, parts_ref, out_ref, *spec_refs):
-    windows, rows, zs, blocks, half = dims
+    )(*[
+        pltpu.with_memory_space_constraint(a, pltpu.HBM)
+        for a in (live_mask, raw_strain, fir_taps[None, :], band_bins[None, :])
+    ])
+
+
+def rows_kernel(dims, parts_ref, out_ref, turned_ref):
+    windows, rows, zs, half, per_group, pack = dims
     height = rows * zs
-    width = height * blocks
+    own = lax.axis_index("freq")
+    lane = iota((height, 2 * half), 1)
+    depth = 2 * windows
+    blank = jnp.zeros((LANES - 2 * height, 2 * half), F32)
+    for pair in range(0, windows, 2):
+        mine = ([], [])
+        for z in range(zs):
+            slot = lax.rem(own + zs - z, zs)
+            got = parts_ref[slot, pair * rows : (pair + 2) * rows, :].astype(F32)
+            mine[0].append(got[:rows])
+            mine[1].append(got[rows:])
+        for e in range(2):
+            straight = jnp.concatenate(mine[e], axis=0)
+            swapped = pltpu.roll(straight, half, 1)
+            swapped = jnp.where(lane < half, swapped, -swapped)
+            flipped = jnp.concatenate([straight, swapped, blank], axis=0).T
+            for part in range(2):
+                turned_ref[pl.ds(2 * (pair + e) + part, half, stride=depth), :] = flipped[part * half : (part + 1) * half]
+    lane = iota((2 * height, LANES), 1)
+    for group in range(per_group // pack):
+        got = turned_ref[group * pack * depth : (group + 1) * pack * depth, :]
+        got = jnp.concatenate([got, jnp.zeros((LANES - pack * depth, LANES), F32)], axis=0).T[: 2 * height]
+        for k in range(pack):
+            inside = (lane >= k * depth) & (lane < (k + 1) * depth)
+            out_ref[group, k * 2 * height : (k + 1) * 2 * height, :] = jnp.where(inside, got, 0.0).astype(BF16)
+
+
+def correlate_kernel(dims, left_ref, parts_ref, out_hbm, *refs):
+    windows, rows, zs, blocks, half, per_group, pack = dims
+    *spec_refs, out_ref, sems = refs
+    height = rows * zs
+    depth = 2 * windows
     block = lax.axis_index("chan")
-    z_own = lax.axis_index("freq")
-
-    @pl.when(pl.program_id(0) == 0)
-    def _():
-        lane = iota((height, 2 * half), 1)
-        for pair in range(0, windows, 2):
-            at = pair * rows
+    own = lax.axis_index("freq")
+    per_tile = LANES // height
+    for pair in range(0, windows, 2):
+        for tile, spec_ref in enumerate(spec_refs):
             slabs = ([], [])
-            for b in range(blocks):
+            for b in range(tile * per_tile, (tile + 1) * per_tile):
                 for z in range(zs):
-                    got = parts_ref[block ^ b, z_own ^ z, at : at + 2 * rows, :].astype(F32)
+                    slot = lax.rem(own + zs - z, zs)
+                    got = parts_ref[(block ^ b) & 1, (block ^ b) >> 1, slot, pair * rows : (pair + 2) * rows, :].astype(F32)
                     slabs[0].append(got[:rows])
                     slabs[1].append(got[rows:])
-            mine = ([], [])
-            for z in range(zs):
-                got = parts_ref[0, z_own ^ z, at : at + 2 * rows, :].astype(F32)
-                mine[0].append(got[:rows])
-                mine[1].append(got[rows:])
             for e in range(2):
-                own = jnp.concatenate(mine[e], axis=0)
-                turned = jnp.where(lane < half, pltpu.roll(own, half, 1), -pltpu.roll(own, half, 1))
-                tail = jnp.zeros((up(2 * height, LANES) - 2 * height, 2 * half), F32)
-                full = jnp.concatenate(slabs[e] + [own, turned, tail], axis=0)
-                start = 2 * half * (pair + e)
-                for r in range(0, full.shape[0], LANES):
-                    spec_refs[r // LANES][start : start + 2 * half, :] = full[r : r + LANES].T
-
-    first = pl.program_id(0) * step_bins
-    for k in range(step_bins):
-        got = [ref[pl.ds(first + k, 2 * windows, stride=half), :] for ref in spec_refs]
-        got = jnp.concatenate(got, axis=1).astype(BF16)
-        prod = lax.dot_general(
-            got[:, width : width + 2 * height], got[:, :width],
-            (((0,), (0,)), ((), ())), preferred_element_type=F32,
-        ) * F32(1.0 / windows)
-        out_ref[k, 0] = prod[:height]
-        out_ref[k, 1] = prod[height:]
-
-
-def correlate(parts, per_group, rows):
-    blocks, zs, full_rows, lanes = parts.shape
+                flipped = jnp.concatenate(slabs[e], axis=0).T
+                for part in range(2):
+                    spec_ref[pl.ds(2 * (pair + e) + part, half, stride=depth), :] = flipped[part * half : (part + 1) * half]
+    copies = []
+    for group in range(per_group // pack):
+        at = group * pack * depth
+        right = [ref[at : at + pack * depth, :] for ref in spec_refs]
+        right = jnp.concatenate(right, axis=1).astype(BF16)
+        prod = jnp.dot(left_ref[group, :, : pack * depth], right, preferred_element_type=F32)
+        prod = prod * F32(1.0 / windows)
+        first = group * pack
+        out_ref[first : first + pack] = prod.reshape(pack, 2, height, prod.shape[1])
+        copies.append(pltpu.make_async_copy(out_ref.at[pl.ds(first, pack)], out_hbm.at[pl.ds(first, pack)], sems.at[group]))
+        copies[-1].start()
+    for each in copies:
+        each.wait()
+
+
+def pack_of(per_group, windows):
+    return next(p for p in (4, 2, 1) if per_group % p == 0 and 2 * windows * p <= LANES)
+
+
+def row_side(parts, per_group, rows):
+    zs, full_rows, lanes = parts.shape
+    windows = full_rows // rows
+    pack = pack_of(per_group, windows)
+    half = lanes // 2
+    height = rows * zs
+    vmem = pl.BlockSpec(memory_space=pltpu.VMEM)
+    return pl.pallas_call(
+        functools.partial(rows_kernel, (windows, rows, zs, half, per_group, pack)),
+        out_shape=jax.ShapeDtypeStruct((per_group // pack, pack * 2 * height, LANES), BF16),
+        in_specs=[vmem],
+        out_specs=vmem,
+        scratch_shapes=[pltpu.VMEM((half * 2 * windows, LANES), F32)],
+        compiler_params=pltpu.CompilerParams(vmem_limit_bytes=8 << 20),
+        cost_estimate=pl.CostEstimate(flops=1 << 24, bytes_accessed=4 << 20, transcendentals=0),
+        name="rows",
+    )(parts)
+
+
+def correlate(left, parts, per_group, rows):
+    _, chips, zs, full_rows, lanes = parts.shape
+    blocks = 2 * chips
     windows = full_rows // rows
     half = lanes // 2
     height = rows * zs
     width = height * blocks
-    step_bins = next(s for s in (10, 6, 5, 4, 3, 2, 1) if per_group % s == 0)
-    dims = (windows, rows, zs, blocks, half)
+    pack = pack_of(per_group, windows)
+    dims = (windows, rows, zs, blocks, half, per_group, pack)
+    vmem = pl.BlockSpec(memory_space=pltpu.VMEM)
+    shape = (per_group, 2, height, width)
     return pl.pallas_call(
-        functools.partial(correlate_kernel, dims, step_bins),
-        grid=(per_group // step_bins,),
-        out_shape=jax.ShapeDtypeStruct((per_group, 2, height, width), F32),
-        in_specs=[pl.BlockSpec(memory_space=pltpu.VMEM)],
-        out_specs=pl.BlockSpec((step_bins, 2, height, width), lambda i: (i, 0, 0, 0)),
-        scratch_shapes=[pltpu.VMEM((windows * 2 * half, LANES), F32)]
-        * ((width + up(2 * height, LANES)) // LANES),
-        compiler_params=pltpu.CompilerParams(vmem_limit_bytes=16 << 20),
+        functools.partial(correlate_kernel, dims),
+        out_shape=jax.ShapeDtypeStruct(shape, F32),
+        in_specs=[vmem, vmem],
+        out_specs=pl.BlockSpec(memory_space=pltpu.HBM),
+        scratch_shapes=[pltpu.VMEM((half * 2 * windows, LANES), F32)] * (width // LANES)
+        + [pltpu.VMEM(shape, F32), pltpu.SemaphoreType.DMA((per_group // pack,))],
+        compiler_params=pltpu.CompilerParams(vmem_limit_bytes=(24 if blocks <= 8 else 44) << 20),
         name="correlate",
-    )(parts)
+    )(left, parts)
 
 
 def shards(groups, blocks, raw_strain, fir_taps, band_bins, live_mask):
@@ -282,26 +338,18 @@
     per_group = band_bins.shape[0] // groups
     pieces = front(raw_strain, fir_taps, band_bins, live_mask, groups)
     got = [pieces[0]]
-    for slot in range(groups - 1, 0, -1):
-        pairs = [(i, i ^ slot) for i in range(groups)]
-        got.insert(1, lax.ppermute(pieces[slot], "freq", pairs))
-    parts = jnp.stack(got)[None]
-    step = 2
-    order = []
-    while step < blocks:
-        order.append(step)
-        step *= 2
-    order.append(1)
-    slots = [0]
-    held = {0: parts}
-    for step in order:
-        base = jnp.concatenate([held[s] for s in slots], axis=0) if len(slots) > 1 else held[slots[0]]
-        moved = lax.ppermute(base, "chan", [(i, i ^ step) for i in range(blocks)])
-        for n, s in enumerate(list(slots)):
-            held[s ^ step] = moved[n : n + 1]
-            slots.append(s ^ step)
-    parts = jnp.concatenate([held[s] for s in range(blocks)], axis=0)
-    return correlate(parts, per_group, rows)
+    for slot in range(1, groups):
+        pairs = [(i, (i + slot) % groups) for i in range(groups)]
+        got.append(lax.ppermute(pieces[slot], "freq", pairs))
+    parts = jnp.stack(got)
+    left = row_side(parts, per_group, rows)
+    same = [parts[None]]
+    for step in range(2, blocks, 2):
+        same.append(lax.ppermute(parts[None], "chan", [(i, i ^ step) for i in range(blocks)]))
+    same = jnp.concatenate(same, axis=0)
+    other = lax.ppermute(same, "chan", [(i, i ^ 1) for i in range(blocks)])
+    both = jnp.stack([same, other])
+    return correlate(left, both, per_group, rows)
 
 
 def solution(mesh):

time: 35.7 us -> 25.7 us (0.72)
  waiting for transfers between devices: 13.9 us -> 7.42 us
  local copies, waits for them, and re-layouts: 3.77 us -> 0 us
  starting transfers between devices: 8.92 us -> 10.7 us
  Pallas kernels: 8.72 us -> 7.33 us
    ppermute x6 -> x7, waiting for transfers between devices: 13.9 us -> 7.42 us  [the longest x3 3.91 us: shards(): lax.ppermute(parts[None], 'chan', [(i, i ^ step) for i in range(blocks)])]
    unnamed x14 -> x0, local copies, waits for them, and re-layouts: 3.76 us -> none
    ppermute x6 -> x7, starting transfers between devices: 8.92 us -> 10.7 us  [the longest x3 7.04 us: shards(): got.append(lax.ppermute(pieces[slot], 'freq', pairs))]
    pallas_call x1 -> x2, Pallas kernels: 4.45 us -> 2.99 us  [the longest x1 2.47 us: correlate(): pl.pallas_call(functools.partial(correlate_kernel, dims), out_shape=jax.S...]
  transfers between devices with their start and end apart: 6 -> 7, of which waited for: 5 -> 6; matrix products, arithmetic and copies ran while one was open for 0% -> 0% of each run, Pallas kernels for 0% -> 2%
where the time goes in v2:
time: 25.7 us; the launch traced here: 25.6 us
  starting transfers between devices  10.7 us (42%)
  waiting for transfers between devices  7.42 us (29%)
  Pallas kernels  7.33 us (29%)
    ppermute x3, starting transfers between devices, shards(): got.append(lax.ppermute(pieces[slot], 'freq', pairs))  7.04 us
    pallas_call x1, Pallas kernels, front(): pl.pallas_call(functools.partial(front_kernel, dims), out_shape=[jax.Shap...  4.33 us
    ppermute x3, waiting for transfers between devices, shards(): lax.ppermute(parts[None], 'chan', [(i, i ^ step) for i in range(blocks)])  3.91 us
    ppermute x3, starting transfers between devices, shards(): lax.ppermute(parts[None], 'chan', [(i, i ^ step) for i in range(blocks)])  3.55 us
    pallas_call x1, Pallas kernels, correlate(): pl.pallas_call(functools.partial(correlate_kernel, dims), out_shape=jax.S...  2.47 us
    ppermute x3, waiting for transfers between devices, shards(): got.append(lax.ppermute(pieces[slot], 'freq', pairs))  2.43 us
    ppermute x1, waiting for transfers between devices, shards(): other = lax.ppermute(same, 'chan', [(i, i ^ 1) for i in range(blocks)])  1.08 us
    pallas_call x1, Pallas kernels, row_side(): pl.pallas_call(functools.partial(rows_kernel, (windows, rows, zs, half, p...  0.53 us
  transfers between devices with their start and end apart: 7, of which 6 were waited for; matrix products, arithmetic and copies ran while one was open for 0% of the time, Pallas kernels for 2%

profile of v2, /device:TPU:0, one launch (start us, length us, event | category | flops | bytes accessed | tf_op | source)
XLA Modules:
  0.0 25.6 jit_solution(17260752191697835880)
XLA Ops:
  0.0 4.3 %front.1 = (bf16[80,128]{1,0:T(8,128)(2,1)S(1)}, bf16[80,128]{1,0:T(8,128)(2,1)S(1)}, bf16[80,128]{1,0:T(8,128)(2,1)S(1)}, bf16[80,128]{1,0:T(8,128)(2,1)S(1)}) custom-call(s32[1,8]{1,0:T(1,128)} %mask_hbm.1, bf16[1,8,150000]{2,1,0:T(8,128)(2,1)} %x_hbm.1, bf16[1,20]{1,0:T(2,128)(2,1)} %bitcast.17, s32[1,240]{1,0:T(1,128)} %bitcast.16), custom_call_target="tpu_custom_call" | custom-call | tf_op jit(solution)/shard_map/front/pallas_call | solution.py:200
  4.3 3.1 %collective-permute-start = (bf16[80,128]{1,0:T(8,128)(2,1)S(1)}, bf16[80,128]{1,0:T(8,128)(2,1)S(1)}, u32[]{:S(2)}, u32[]{:S(2)}) collective-permute-start(bf16[80,128]{1,0:T(8,128)(2,1)S(1)} %get-tuple-element.10), channel_id=1, source_target_pairs={{0,8},{8,16},{16,24},{24,0},{1,9},{9,17},{17,25},{25,1},{2,10},{10... | collective-permute-start | bytes 61448 | tf_op jit(solution)/shard_map/ppermute | solution.py:343
  7.4 2.6 %collective-permute-start.1 = (bf16[80,128]{1,0:T(8,128)(2,1)S(1)}, bf16[80,128]{1,0:T(8,128)(2,1)S(1)}, u32[]{:S(2)}, u32[]{:S(2)}) collective-permute-start(bf16[80,128]{1,0:T(8,128)(2,1)S(1)} %get-tuple-element.11), channel_id=1, source_target_pairs={{0,16},{8,24},{16,0},{24,8},{1,17},{9,25},{17,1},{25,9},{2,18},{10... | collective-permute-start | bytes 61448 | tf_op jit(solution)/shard_map/ppermute | solution.py:343
  10.0 1.3 %collective-permute-start.2 = (bf16[80,128]{1,0:T(8,128)(2,1)S(1)}, bf16[80,128]{1,0:T(8,128)(2,1)S(1)}, u32[]{:S(2)}, u32[]{:S(2)}) collective-permute-start(bf16[80,128]{1,0:T(8,128)(2,1)S(1)} %get-tuple-element.12), channel_id=1, source_target_pairs={{0,24},{8,0},{16,8},{24,16},{1,25},{9,1},{17,9},{25,17},{2,26},{10... | collective-permute-start | bytes 61448 | tf_op jit(solution)/shard_map/ppermute | solution.py:343
  11.4 0.0 collective-permute-done
  11.4 0.9 %collective-permute-done.1 = bf16[80,128]{1,0:T(8,128)(2,1)S(1)} collective-permute-done((bf16[80,128]{1,0:T(8,128)(2,1)S(1)}, bf16[80,128]{1,0:T(8,128)(2,1)S(1)}, u32[]{:S(2)}, u32[]{:S(2)}) %collective-permute-start.1) | collective-permute-done | bytes 20512 | tf_op jit(solution)/shard_map/ppermute | solution.py:343
  12.3 1.6 %collective-permute-done.2 = bf16[80,128]{1,0:T(8,128)(2,1)S(1)} collective-permute-done((bf16[80,128]{1,0:T(8,128)(2,1)S(1)}, bf16[80,128]{1,0:T(8,128)(2,1)S(1)}, u32[]{:S(2)}, u32[]{:S(2)}) %collective-permute-start.2) | collective-permute-done | bytes 20512 | tf_op jit(solution)/shard_map/ppermute | solution.py:343
  13.8 2.5 %collective-permute-start.5 = (bf16[1,4,80,128]{3,2,1,0:T(8,128)(2,1)S(1)}, bf16[1,4,80,128]{3,2,1,0:T(8,128)(2,1)S(1)}, u32[]{:S(2)}, u32[]{:S(2)}) collective-permute-start(bf16[1,4,80,128]{3,2,1,0:T(8,128)(2,1)S(1)} %get-tuple-element.15), channel_id=1, source_target_pairs={{0,6},{1,7},{2,4},{3,5},{4,2},{5,3},{6,0},{7,1},{8,14},{9,15},{10,... | collective-permute-start | bytes 245768 | tf_op jit(solution)/shard_map/ppermute | solution.py:348
  16.4 0.5 %collective-permute-start.4 = (bf16[1,4,80,128]{3,2,1,0:T(8,128)(2,1)S(1)}, bf16[1,4,80,128]{3,2,1,0:T(8,128)(2,1)S(1)}, u32[]{:S(2)}, u32[]{:S(2)}) collective-permute-start(bf16[1,4,80,128]{3,2,1,0:T(8,128)(2,1)S(1)} %get-tuple-element.15), channel_id=1, source_target_pairs={{0,4},{1,5},{2,6},{3,7},{4,0},{5,1},{6,2},{7,3},{8,12},{9,13},{10,... | collective-permute-start | bytes 245768 | tf_op jit(solution)/shard_map/ppermute | solution.py:348
  16.9 0.5 %collective-permute-start.3 = (bf16[1,4,80,128]{3,2,1,0:T(8,128)(2,1)S(1)}, bf16[1,4,80,128]{3,2,1,0:T(8,128)(2,1)S(1)}, u32[]{:S(2)}, u32[]{:S(2)}) collective-permute-start(bf16[1,4,80,128]{3,2,1,0:T(8,128)(2,1)S(1)} %get-tuple-element.15), channel_id=1, source_target_pairs={{0,2},{1,3},{2,0},{3,1},{4,6},{5,7},{6,4},{7,5},{8,10},{9,11},{10,... | collective-permute-start | bytes 245768 | tf_op jit(solution)/shard_map/ppermute | solution.py:348
  17.4 2.8 %collective-permute-done.5 = bf16[1,4,80,128]{3,2,1,0:T(8,128)(2,1)S(1)} collective-permute-done((bf16[1,4,80,128]{3,2,1,0:T(8,128)(2,1)S(1)}, bf16[1,4,80,128]{3,2,1,0:T(8,128)(2,1)S(1)}, u32[]{:S(2)}, u32[]{:S(2)}) %collective-permute-start.5) | collective-permute-done | bytes 81952 | tf_op jit(solution)/shard_map/ppermute | solution.py:348
  20.2 0.7 %collective-permute-done.4 = bf16[1,4,80,128]{3,2,1,0:T(8,128)(2,1)S(1)} collective-permute-done((bf16[1,4,80,128]{3,2,1,0:T(8,128)(2,1)S(1)}, bf16[1,4,80,128]{3,2,1,0:T(8,128)(2,1)S(1)}, u32[]{:S(2)}, u32[]{:S(2)}) %collective-permute-start.4) | collective-permute-done | bytes 81952 | tf_op jit(solution)/shard_map/ppermute | solution.py:348
  20.9 0.4 %collective-permute-done.3 = bf16[1,4,80,128]{3,2,1,0:T(8,128)(2,1)S(1)} collective-permute-done((bf16[1,4,80,128]{3,2,1,0:T(8,128)(2,1)S(1)}, bf16[1,4,80,128]{3,2,1,0:T(8,128)(2,1)S(1)}, u32[]{:S(2)}, u32[]{:S(2)}) %collective-permute-start.3) | collective-permute-done | bytes 81952 | tf_op jit(solution)/shard_map/ppermute | solution.py:348
  21.3 0.1 fusion.1
  21.4 0.1 collective-permute-start.6
  21.4 0.5 %rows.1.left_ref = bf16[15,256,128]{2,1,0:T(8,128)(2,1)S(1)} custom-call(bf16[4,80,128]{2,1,0:T(8,128)(2,1)S(1)} %get-tuple-element.16.parts_ref), custom_call_target="tpu_custom_call" | custom-call | flops 16777216 | bytes 4194304 | tf_op jit(solution)/shard_map/rows/pallas_call | solution.py:301
  22.0 1.1 %collective-permute-done.6 = bf16[4,4,80,128]{3,2,1,0:T(8,128)(2,1)S(1)} collective-permute-done((bf16[4,4,80,128]{3,2,1,0:T(8,128)(2,1)S(1)}, bf16[4,4,80,128]{3,2,1,0:T(8,128)(2,1)S(1)}, u32[]{:S(2)}, u32[]{:S(2)}) %collective-permute-start.6) | collective-permute-done | bytes 327712 | tf_op jit(solution)/shard_map/ppermute | solution.py:350
  23.1 0.1 pad_maximum_fusion.parts_ref
  23.1 2.5 %correlate.1 = f32[60,2,32,256]{3,2,1,0:T(8,128)} custom-call(bf16[15,256,128]{2,1,0:T(8,128)(2,1)S(1)} %rows.1.left_ref, bf16[2,4,4,80,128]{4,3,2,1,0:T(8,128)(2,1)S(1)} %pad_maximum_fusion.parts_ref), custom_call_target="tpu_custom_call" | custom-call | tf_op jit(solution)/shard_map/correlate/pallas_call | solution.py:324
  (1 shorter events, 0.0 us)
Async XLA Ops:
  4.3 7.0 %collective-permute-start = (bf16[80,128]{1,0:T(8,128)(2,1)S(1)}, bf16[80,128]{1,0:T(8,128)(2,1)S(1)}, u32[]{:S(2)}, u32[]{:S(2)}) collective-permute-start(bf16[80,128]{1,0:T(8,128)(2,1)S(1)} %get-tuple-element.10), channel_id=1, source_target_pairs={{0,8},{8,16},{16,24},{24,0},{1,9},{9,17},{17,25},{25,1},{2,10},{10... | collective-permute-start | bytes 61448 | tf_op jit(solution)/shard_map/ppermute | solution.py:343
  7.4 4.8 %collective-permute-start.1 = (bf16[80,128]{1,0:T(8,128)(2,1)S(1)}, bf16[80,128]{1,0:T(8,128)(2,1)S(1)}, u32[]{:S(2)}, u32[]{:S(2)}) collective-permute-start(bf16[80,128]{1,0:T(8,128)(2,1)S(1)} %get-tuple-element.11), channel_id=1, source_target_pairs={{0,16},{8,24},{16,0},{24,8},{1,17},{9,25},{17,1},{25,9},{2,18},{10... | collective-permute-start | bytes 61448 | tf_op jit(solution)/shard_map/ppermute | solution.py:343
  10.0 3.8 %collective-permute-start.2 = (bf16[80,128]{1,0:T(8,128)(2,1)S(1)}, bf16[80,128]{1,0:T(8,128)(2,1)S(1)}, u32[]{:S(2)}, u32[]{:S(2)}) collective-permute-start(bf16[80,128]{1,0:T(8,128)(2,1)S(1)} %get-tuple-element.12), channel_id=1, source_target_pairs={{0,24},{8,0},{16,8},{24,16},{1,25},{9,1},{17,9},{25,17},{2,26},{10... | collective-permute-start | bytes 61448 | tf_op jit(solution)/shard_map/ppermute | solution.py:343
  13.8 6.3 %collective-permute-start.5 = (bf16[1,4,80,128]{3,2,1,0:T(8,128)(2,1)S(1)}, bf16[1,4,80,128]{3,2,1,0:T(8,128)(2,1)S(1)}, u32[]{:S(2)}, u32[]{:S(2)}) collective-permute-start(bf16[1,4,80,128]{3,2,1,0:T(8,128)(2,1)S(1)} %get-tuple-element.15), channel_id=1, source_target_pairs={{0,6},{1,7},{2,4},{3,5},{4,2},{5,3},{6,0},{7,1},{8,14},{9,15},{10,... | collective-permute-start | bytes 245768 | tf_op jit(solution)/shard_map/ppermute | solution.py:348
  16.4 4.5 %collective-permute-start.4 = (bf16[1,4,80,128]{3,2,1,0:T(8,128)(2,1)S(1)}, bf16[1,4,80,128]{3,2,1,0:T(8,128)(2,1)S(1)}, u32[]{:S(2)}, u32[]{:S(2)}) collective-permute-start(bf16[1,4,80,128]{3,2,1,0:T(8,128)(2,1)S(1)} %get-tuple-element.15), channel_id=1, source_target_pairs={{0,4},{1,5},{2,6},{3,7},{4,0},{5,1},{6,2},{7,3},{8,12},{9,13},{10,... | collective-permute-start | bytes 245768 | tf_op jit(solution)/shard_map/ppermute | solution.py:348
  16.9 4.4 %collective-permute-start.3 = (bf16[1,4,80,128]{3,2,1,0:T(8,128)(2,1)S(1)}, bf16[1,4,80,128]{3,2,1,0:T(8,128)(2,1)S(1)}, u32[]{:S(2)}, u32[]{:S(2)}) collective-permute-start(bf16[1,4,80,128]{3,2,1,0:T(8,128)(2,1)S(1)} %get-tuple-element.15), channel_id=1, source_target_pairs={{0,2},{1,3},{2,0},{3,1},{4,6},{5,7},{6,4},{7,5},{8,10},{9,11},{10,... | collective-permute-start | bytes 245768 | tf_op jit(solution)/shard_map/ppermute | solution.py:348
  21.4 1.7 %collective-permute-start.6 = (bf16[4,4,80,128]{3,2,1,0:T(8,128)(2,1)S(1)}, bf16[4,4,80,128]{3,2,1,0:T(8,128)(2,1)S(1)}, u32[]{:S(2)}, u32[]{:S(2)}) collective-permute-start(bf16[4,4,80,128]{3,2,1,0:T(8,128)(2,1)S(1)} %get-tuple-element.14), channel_id=1, source_target_pairs={{0,1},{1,0},{2,3},{3,2},{4,5},{5,4},{6,7},{7,6},{8,9},{9,8},{10,11... | collective-permute-start | bytes 983048 | tf_op jit(solution)/shard_map/ppermute | solution.py:350

commit v3 on v2

--- a/solution.py
+++ b/solution.py
@@ -55,24 +55,43 @@
     ]
     for each in small:
         each.start()
-    copy = pltpu.make_async_copy(x_hbm.at[0], x_ref, sems.at[3])
-    copy.start()
-    for each in small:
-        each.wait()
+    total = x_ref.shape[1]
     width = groups * 2 * half
     chunk = factor * LANES
     tiles = factor + 1
     tap_count = taps_ref.shape[1]
-
+    chunks = -(-total // chunk)
+    stages = sems.shape[0] - len(small)
+    cuts = [up(chunks * k // stages, 2) for k in range(stages)] + [chunks]
+    loads = []
+    for k in range(stages):
+        begin, end = cuts[k] * chunk, min(cuts[k + 1] * chunk, total)
+        span = (0, slice(None), pl.ds(begin, end - begin))
+        loads.append(pltpu.make_async_copy(x_hbm.at[span], x_ref.at[span[1:]], sems.at[len(small) + k]))
+        loads[-1].start()
+    for each in small:
+        each.wait()
+
+    period = math.lcm(SUB, factor)
+    middle = LANES // 2
     taps = jnp.concatenate([taps_ref[...].astype(F32), jnp.zeros((1, LANES - tap_count), F32)], axis=1)
     taps = jnp.broadcast_to(taps, (SUB, LANES))
-    base = factor * iota((SUB, LANES), 1) + (factor - 1 + LANES) - iota((SUB, LANES), 0)
+    lane8 = iota((SUB, LANES), 1)
+    seeds = []
+    for start in range(0, period, SUB):
+        tap = factor * (lane8 - middle) + (factor - 1 + LANES - start) - iota((SUB, LANES), 0)
+        tap = jnp.where((tap >= 0) & (tap < tap_count), tap, LANES - 1)
+        seeds.append(jnp.take_along_axis(taps, tap, axis=1, mode="promise_in_bounds"))
     for row in range(0, tiles * LANES, 2 * SUB):
         pair = []
         for start in (row, row + SUB):
-            tap = base - start
-            tap = jnp.where((tap >= 0) & (tap < tap_count), tap, LANES - 1)
-            pair.append(jnp.take_along_axis(taps, tap, axis=1, mode="promise_in_bounds"))
+            moved = start // period * (period // factor)
+            block = pltpu.roll(seeds[start % period // SUB], (moved - middle) % LANES, 1)
+            if moved < 2 * SUB:
+                block = jnp.where(lane8 < middle, block, 0.0)
+            elif moved > LANES - 2 * SUB:
+                block = jnp.where(lane8 >= middle, block, 0.0)
+            pair.append(block)
         band_ref[row : row + 2 * SUB, :] = jnp.concatenate(pair, axis=0).astype(BF16)
 
     own = lax.axis_index("freq")
@@ -84,48 +103,46 @@
     bins = jnp.broadcast_to(bins, (SUB, held))
     lane = iota((SUB, 2 * half), 1)
     is_imag = lane >= half
-    columns = []
+    valid = (lane & (half - 1)) < per_group
+    blocks = up(length, 2 * LANES) // LANES
+    pairs = blocks // 2
+    row8 = iota((SUB, 2 * half), 0)
+    table_parts = []
     for slot in range(groups):
         first = lax.rem(own + slot, groups) * per_group
         real = pltpu.roll(bins, lax.rem(held - first, held), 1)[:, : 2 * half]
         imag = pltpu.roll(bins, lax.rem(held - first + half, held), 1)[:, : 2 * half]
-        columns.append(jnp.where(is_imag, imag, real))
-    blocks = up(length, LANES) // LANES
-    steps = iota((up(blocks, SUB), 2 * half), 0)
-    valid = (lane & (half - 1)) < per_group
-    for slot in range(groups):
-        bins8 = columns[slot]
-        turn_rows = [
-            cos_sin(wrap((steps[r : r + SUB] * LANES) * bins8, length), length)
-            for r in range(0, steps.shape[0], SUB)
-        ]
-        for row in range(0, LANES, 2 * SUB):
-            here = []
-            for start in (row, row + SUB):
-                c, s = cos_sin(wrap((iota((SUB, 2 * half), 0) + start) * bins8, length), length)
-                here.append((
-                    jnp.where(valid, jnp.where(is_imag, -s, c), 0.0),
-                    jnp.where(valid, jnp.where(is_imag, -c, -s), 0.0),
-                ))
-            for block in range(blocks):
-                turn_c, turn_s = turn_rows[block // SUB]
-                at = block % SUB
-                turn_c, turn_s = turn_c[at : at + 1], turn_s[at : at + 1]
-                value = [v * turn_c + w * turn_s for v, w in here]
+        bins8 = jnp.where(is_imag, imag, real)
+        c, s = cos_sin(wrap((row8 + (blocks - 1) * LANES // 2) * bins8, length), length)
+        near = jnp.where(valid, jnp.where(is_imag, -s, c), 0.0), jnp.where(valid, jnp.where(is_imag, -c, -s), 0.0)
+        rise = [cos_sin(wrap((row8 + r) * SUB * bins8, length), length) for r in range(0, LANES // SUB, SUB)]
+        apart = [cos_sin(wrap((2 * (row8 + r) + 1) * (LANES // 2) * bins8, length), length) for r in range(0, pairs, SUB)]
+        table_parts.append((near, rise, apart))
+
+    def table_rows(slot, row):
+        (near_v, near_w), rise, apart = table_parts[slot]
+        here = []
+        for start in (row // SUB, row // SUB + 1):
+            turn_c, turn_s = (t[start % SUB : start % SUB + 1] for t in rise[start // SUB])
+            here.append((near_v * turn_c + near_w * turn_s, near_w * turn_c - near_v * turn_s))
+        here = [jnp.concatenate(h, axis=0) for h in zip(*here)]
+        for d in range(pairs):
+            turn_c, turn_s = (t[d % SUB : d % SUB + 1] for t in apart[d // SUB])
+            even, odd = here[0] * turn_c, here[1] * turn_s
+            for block, value in ((pairs + d, even + odd), (pairs - 1 - d, even - odd)):
                 table_ref[
                     block * LANES + row : block * LANES + row + 2 * SUB,
                     slot * 2 * half : (slot + 1) * 2 * half,
-                ] = jnp.concatenate(value, axis=0).astype(BF16)
-
-    copy.wait()
-    total = x_ref.shape[1]
-    chunks = -(-total // chunk)
-    entries = [(q, 0) for q in range(chunks)]
+                ] = value.astype(BF16)
+
+    todo = [(slot, row) for slot in range(groups) for row in range(0, LANES, 2 * SUB)]
+
+    entries = [(q, 0) for q in range(up(chunks, 2))]
     for w in range(1, windows):
         begin = w * length * factor
         entries.append((begin // chunk, begin))
+    edge = up(chunks, 2) - 1
     zero_tile = jnp.zeros((rows, LANES), F32)
-    lane8 = iota((rows, LANES), 1)
 
     def tile_of(entry, tile):
         q, begin = entry
@@ -141,14 +158,23 @@
         return got
 
     if len(entries) % 2:
-        entries.append((chunks, 0))
-    for pair in range(0, len(entries), 2):
-        for tile in range(tiles):
-            both = [tile_of(entries[pair + e], tile) for e in range(2)]
-            lhs_ref[pair * rows : (pair + 2) * rows, tile * LANES : (tile + 1) * LANES] = (
-                jnp.concatenate(both, axis=0).astype(BF16)
-            )
-    dec_ref[...] = jnp.dot(lhs_ref[:, 0 : tiles * LANES], band_ref[...], preferred_element_type=F32)
+        entries.append((chunks + 1, 0))
+    bounds = cuts[:-1] + [len(entries)]
+    share = -(-len(todo) // (stages + 1))
+    for slot, row in todo[:share]:
+        table_rows(slot, row)
+    for k in range(stages):
+        loads[k].wait()
+        for pair in range(bounds[k], bounds[k + 1], 2):
+            for tile in range(tiles):
+                both = [tile_of(entries[pair + e], tile) for e in range(2)]
+                lhs_ref[pair * rows : (pair + 2) * rows, tile * LANES : (tile + 1) * LANES] = (
+                    jnp.concatenate(both, axis=0).astype(BF16)
+                )
+        span = slice(bounds[k] * rows, bounds[k + 1] * rows)
+        dec_ref[span, :] = jnp.dot(lhs_ref[span, 0 : tiles * LANES], band_ref[...], preferred_element_type=F32)
+        for slot, row in todo[(k + 1) * share : (k + 2) * share]:
+            table_rows(slot, row)
 
     def dec(entry):
         return dec_ref[entry * rows : (entry + 1) * rows, :]
@@ -159,7 +185,7 @@
         for w in range(windows):
             first, lead = divmod(w * length, LANES)
             entry = first + block
-            low = dec(chunks + w - 1) if (block == 0 and w > 0) else dec(entry)
+            low = dec(edge + w) if (block == 0 and w > 0) else dec(entry)
             if lead:
                 low = pltpu.roll(low, LANES - lead, 1)
                 if entry + 1 < chunks:
@@ -194,8 +220,9 @@
     width = groups * 2 * half
     total = raw_strain.shape[2]
     chunks = -(-total // (DECIM * LANES))
-    entries = up(chunks + WIN - 1, 2)
-    blocks = up(NT, LANES)
+    entries = up(up(chunks, 2) + WIN - 1, 2)
+    blocks = up(NT, 2 * LANES)
+    stages = 4
     vmem = pl.BlockSpec(memory_space=pltpu.VMEM)
     return pl.pallas_call(
         functools.partial(front_kernel, dims),
@@ -211,7 +238,7 @@
             pltpu.VMEM((blocks, width), BF16),
             pltpu.VMEM((entries * rows, max((DECIM + 1) * LANES, blocks)), BF16),
             pltpu.VMEM((entries * rows, LANES), F32),
-            pltpu.SemaphoreType.DMA((4,)),
+            pltpu.SemaphoreType.DMA((3 + stages,)),
         ],
         compiler_params=pltpu.CompilerParams(vmem_limit_bytes=20 << 20),
         name="front",

time: 25.7 us -> 25.2 us (0.981)
  Pallas kernels: 7.33 us -> 6.81 us
    pallas_call x1, Pallas kernels: 4.33 us -> 3.82 us  [front(): pl.pallas_call(functools.partial(front_kernel, dims), out_shape=[jax.Shap...]
where the time goes in v3:
time: 25.2 us; the launch traced here: 25.1 us
  starting transfers between devices  10.7 us (42%)
  waiting for transfers between devices  7.42 us (29%)
  Pallas kernels  6.81 us (27%)
    ppermute x3, starting transfers between devices, shards(): got.append(lax.ppermute(pieces[slot], 'freq', pairs))  7.04 us
    ppermute x3, waiting for transfers between devices, shards(): lax.ppermute(parts[None], 'chan', [(i, i ^ step) for i in range(blocks)])  3.91 us
    pallas_call x1, Pallas kernels, front(): pl.pallas_call(functools.partial(front_kernel, dims), out_shape=[jax.Shap...  3.82 us
    ppermute x3, starting transfers between devices, shards(): lax.ppermute(parts[None], 'chan', [(i, i ^ step) for i in range(blocks)])  3.55 us
    pallas_call x1, Pallas kernels, correlate(): pl.pallas_call(functools.partial(correlate_kernel, dims), out_shape=jax.S...  2.46 us
    ppermute x3, waiting for transfers between devices, shards(): got.append(lax.ppermute(pieces[slot], 'freq', pairs))  2.43 us
    ppermute x1, waiting for transfers between devices, shards(): other = lax.ppermute(same, 'chan', [(i, i ^ 1) for i in range(blocks)])  1.08 us
    pallas_call x1, Pallas kernels, row_side(): pl.pallas_call(functools.partial(rows_kernel, (windows, rows, zs, half, p...  0.53 us
  transfers between devices with their start and end apart: 7, of which 6 were waited for; matrix products, arithmetic and copies ran while one was open for 0% of the time, Pallas kernels for 2%

profile of v3, /device:TPU:0, one launch (start us, length us, event | category | flops | bytes accessed | tf_op | source)
XLA Modules:
  0.0 25.1 jit_solution(5022190895800702173)
XLA Ops:
  0.0 3.8 %front.1 = (bf16[80,128]{1,0:T(8,128)(2,1)S(1)}, bf16[80,128]{1,0:T(8,128)(2,1)S(1)}, bf16[80,128]{1,0:T(8,128)(2,1)S(1)}, bf16[80,128]{1,0:T(8,128)(2,1)S(1)}) custom-call(s32[1,8]{1,0:T(1,128)} %mask_hbm.1, bf16[1,8,150000]{2,1,0:T(8,128)(2,1)} %x_hbm.1, bf16[1,20]{1,0:T(2,128)(2,1)} %bitcast.17, s32[1,240]{1,0:T(1,128)} %bitcast.16), custom_call_target="tpu_custom_call" | custom-call | tf_op jit(solution)/shard_map/front/pallas_call | solution.py:227
  3.8 3.1 %collective-permute-start = (bf16[80,128]{1,0:T(8,128)(2,1)S(1)}, bf16[80,128]{1,0:T(8,128)(2,1)S(1)}, u32[]{:S(2)}, u32[]{:S(2)}) collective-permute-start(bf16[80,128]{1,0:T(8,128)(2,1)S(1)} %get-tuple-element.10), channel_id=1, source_target_pairs={{0,8},{8,16},{16,24},{24,0},{1,9},{9,17},{17,25},{25,1},{2,10},{10... | collective-permute-start | bytes 61448 | tf_op jit(solution)/shard_map/ppermute | solution.py:370
  6.9 2.6 %collective-permute-start.1 = (bf16[80,128]{1,0:T(8,128)(2,1)S(1)}, bf16[80,128]{1,0:T(8,128)(2,1)S(1)}, u32[]{:S(2)}, u32[]{:S(2)}) collective-permute-start(bf16[80,128]{1,0:T(8,128)(2,1)S(1)} %get-tuple-element.11), channel_id=1, source_target_pairs={{0,16},{8,24},{16,0},{24,8},{1,17},{9,25},{17,1},{25,9},{2,18},{10... | collective-permute-start | bytes 61448 | tf_op jit(solution)/shard_map/ppermute | solution.py:370
  9.5 1.3 %collective-permute-start.2 = (bf16[80,128]{1,0:T(8,128)(2,1)S(1)}, bf16[80,128]{1,0:T(8,128)(2,1)S(1)}, u32[]{:S(2)}, u32[]{:S(2)}) collective-permute-start(bf16[80,128]{1,0:T(8,128)(2,1)S(1)} %get-tuple-element.12), channel_id=1, source_target_pairs={{0,24},{8,0},{16,8},{24,16},{1,25},{9,1},{17,9},{25,17},{2,26},{10... | collective-permute-start | bytes 61448 | tf_op jit(solution)/shard_map/ppermute | solution.py:370
  10.9 0.0 collective-permute-done
  10.9 0.9 %collective-permute-done.1 = bf16[80,128]{1,0:T(8,128)(2,1)S(1)} collective-permute-done((bf16[80,128]{1,0:T(8,128)(2,1)S(1)}, bf16[80,128]{1,0:T(8,128)(2,1)S(1)}, u32[]{:S(2)}, u32[]{:S(2)}) %collective-permute-start.1) | collective-permute-done | bytes 20512 | tf_op jit(solution)/shard_map/ppermute | solution.py:370
  11.8 1.6 %collective-permute-done.2 = bf16[80,128]{1,0:T(8,128)(2,1)S(1)} collective-permute-done((bf16[80,128]{1,0:T(8,128)(2,1)S(1)}, bf16[80,128]{1,0:T(8,128)(2,1)S(1)}, u32[]{:S(2)}, u32[]{:S(2)}) %collective-permute-start.2) | collective-permute-done | bytes 20512 | tf_op jit(solution)/shard_map/ppermute | solution.py:370
  13.3 2.5 %collective-permute-start.5 = (bf16[1,4,80,128]{3,2,1,0:T(8,128)(2,1)S(1)}, bf16[1,4,80,128]{3,2,1,0:T(8,128)(2,1)S(1)}, u32[]{:S(2)}, u32[]{:S(2)}) collective-permute-start(bf16[1,4,80,128]{3,2,1,0:T(8,128)(2,1)S(1)} %get-tuple-element.15), channel_id=1, source_target_pairs={{0,6},{1,7},{2,4},{3,5},{4,2},{5,3},{6,0},{7,1},{8,14},{9,15},{10,... | collective-permute-start | bytes 245768 | tf_op jit(solution)/shard_map/ppermute | solution.py:375
  15.8 0.5 %collective-permute-start.4 = (bf16[1,4,80,128]{3,2,1,0:T(8,128)(2,1)S(1)}, bf16[1,4,80,128]{3,2,1,0:T(8,128)(2,1)S(1)}, u32[]{:S(2)}, u32[]{:S(2)}) collective-permute-start(bf16[1,4,80,128]{3,2,1,0:T(8,128)(2,1)S(1)} %get-tuple-element.15), channel_id=1, source_target_pairs={{0,4},{1,5},{2,6},{3,7},{4,0},{5,1},{6,2},{7,3},{8,12},{9,13},{10,... | collective-permute-start | bytes 245768 | tf_op jit(solution)/shard_map/ppermute | solution.py:375
  16.3 0.5 %collective-permute-start.3 = (bf16[1,4,80,128]{3,2,1,0:T(8,128)(2,1)S(1)}, bf16[1,4,80,128]{3,2,1,0:T(8,128)(2,1)S(1)}, u32[]{:S(2)}, u32[]{:S(2)}) collective-permute-start(bf16[1,4,80,128]{3,2,1,0:T(8,128)(2,1)S(1)} %get-tuple-element.15), channel_id=1, source_target_pairs={{0,2},{1,3},{2,0},{3,1},{4,6},{5,7},{6,4},{7,5},{8,10},{9,11},{10,... | collective-permute-start | bytes 245768 | tf_op jit(solution)/shard_map/ppermute | solution.py:375
  16.9 2.8 %collective-permute-done.5 = bf16[1,4,80,128]{3,2,1,0:T(8,128)(2,1)S(1)} collective-permute-done((bf16[1,4,80,128]{3,2,1,0:T(8,128)(2,1)S(1)}, bf16[1,4,80,128]{3,2,1,0:T(8,128)(2,1)S(1)}, u32[]{:S(2)}, u32[]{:S(2)}) %collective-permute-start.5) | collective-permute-done | bytes 81952 | tf_op jit(solution)/shard_map/ppermute | solution.py:375
  19.7 0.7 %collective-permute-done.4 = bf16[1,4,80,128]{3,2,1,0:T(8,128)(2,1)S(1)} collective-permute-done((bf16[1,4,80,128]{3,2,1,0:T(8,128)(2,1)S(1)}, bf16[1,4,80,128]{3,2,1,0:T(8,128)(2,1)S(1)}, u32[]{:S(2)}, u32[]{:S(2)}) %collective-permute-start.4) | collective-permute-done | bytes 81952 | tf_op jit(solution)/shard_map/ppermute | solution.py:375
  20.4 0.4 %collective-permute-done.3 = bf16[1,4,80,128]{3,2,1,0:T(8,128)(2,1)S(1)} collective-permute-done((bf16[1,4,80,128]{3,2,1,0:T(8,128)(2,1)S(1)}, bf16[1,4,80,128]{3,2,1,0:T(8,128)(2,1)S(1)}, u32[]{:S(2)}, u32[]{:S(2)}) %collective-permute-start.3) | collective-permute-done | bytes 81952 | tf_op jit(solution)/shard_map/ppermute | solution.py:375
  20.8 0.1 fusion.1
  20.8 0.1 collective-permute-start.6
  20.9 0.5 %rows.1.left_ref = bf16[15,256,128]{2,1,0:T(8,128)(2,1)S(1)} custom-call(bf16[4,80,128]{2,1,0:T(8,128)(2,1)S(1)} %get-tuple-element.16.parts_ref), custom_call_target="tpu_custom_call" | custom-call | flops 16777216 | bytes 4194304 | tf_op jit(solution)/shard_map/rows/pallas_call | solution.py:328
  21.5 1.1 %collective-permute-done.6 = bf16[4,4,80,128]{3,2,1,0:T(8,128)(2,1)S(1)} collective-permute-done((bf16[4,4,80,128]{3,2,1,0:T(8,128)(2,1)S(1)}, bf16[4,4,80,128]{3,2,1,0:T(8,128)(2,1)S(1)}, u32[]{:S(2)}, u32[]{:S(2)}) %collective-permute-start.6) | collective-permute-done | bytes 327712 | tf_op jit(solution)/shard_map/ppermute | solution.py:377
  22.5 0.1 pad_maximum_fusion.parts_ref
  22.6 2.5 %correlate.1 = f32[60,2,32,256]{3,2,1,0:T(8,128)} custom-call(bf16[15,256,128]{2,1,0:T(8,128)(2,1)S(1)} %rows.1.left_ref, bf16[2,4,4,80,128]{4,3,2,1,0:T(8,128)(2,1)S(1)} %pad_maximum_fusion.parts_ref), custom_call_target="tpu_custom_call" | custom-call | tf_op jit(solution)/shard_map/correlate/pallas_call | solution.py:351
  (1 shorter events, 0.0 us)
Async XLA Ops:
  3.8 7.0 %collective-permute-start = (bf16[80,128]{1,0:T(8,128)(2,1)S(1)}, bf16[80,128]{1,0:T(8,128)(2,1)S(1)}, u32[]{:S(2)}, u32[]{:S(2)}) collective-permute-start(bf16[80,128]{1,0:T(8,128)(2,1)S(1)} %get-tuple-element.10), channel_id=1, source_target_pairs={{0,8},{8,16},{16,24},{24,0},{1,9},{9,17},{17,25},{25,1},{2,10},{10... | collective-permute-start | bytes 61448 | tf_op jit(solution)/shard_map/ppermute | solution.py:370
  6.9 4.8 %collective-permute-start.1 = (bf16[80,128]{1,0:T(8,128)(2,1)S(1)}, bf16[80,128]{1,0:T(8,128)(2,1)S(1)}, u32[]{:S(2)}, u32[]{:S(2)}) collective-permute-start(bf16[80,128]{1,0:T(8,128)(2,1)S(1)} %get-tuple-element.11), channel_id=1, source_target_pairs={{0,16},{8,24},{16,0},{24,8},{1,17},{9,25},{17,1},{25,9},{2,18},{10... | collective-permute-start | bytes 61448 | tf_op jit(solution)/shard_map/ppermute | solution.py:370
  9.5 3.8 %collective-permute-start.2 = (bf16[80,128]{1,0:T(8,128)(2,1)S(1)}, bf16[80,128]{1,0:T(8,128)(2,1)S(1)}, u32[]{:S(2)}, u32[]{:S(2)}) collective-permute-start(bf16[80,128]{1,0:T(8,128)(2,1)S(1)} %get-tuple-element.12), channel_id=1, source_target_pairs={{0,24},{8,0},{16,8},{24,16},{1,25},{9,1},{17,9},{25,17},{2,26},{10... | collective-permute-start | bytes 61448 | tf_op jit(solution)/shard_map/ppermute | solution.py:370
  13.3 6.3 %collective-permute-start.5 = (bf16[1,4,80,128]{3,2,1,0:T(8,128)(2,1)S(1)}, bf16[1,4,80,128]{3,2,1,0:T(8,128)(2,1)S(1)}, u32[]{:S(2)}, u32[]{:S(2)}) collective-permute-start(bf16[1,4,80,128]{3,2,1,0:T(8,128)(2,1)S(1)} %get-tuple-element.15), channel_id=1, source_target_pairs={{0,6},{1,7},{2,4},{3,5},{4,2},{5,3},{6,0},{7,1},{8,14},{9,15},{10,... | collective-permute-start | bytes 245768 | tf_op jit(solution)/shard_map/ppermute | solution.py:375
  15.8 4.5 %collective-permute-start.4 = (bf16[1,4,80,128]{3,2,1,0:T(8,128)(2,1)S(1)}, bf16[1,4,80,128]{3,2,1,0:T(8,128)(2,1)S(1)}, u32[]{:S(2)}, u32[]{:S(2)}) collective-permute-start(bf16[1,4,80,128]{3,2,1,0:T(8,128)(2,1)S(1)} %get-tuple-element.15), channel_id=1, source_target_pairs={{0,4},{1,5},{2,6},{3,7},{4,0},{5,1},{6,2},{7,3},{8,12},{9,13},{10,... | collective-permute-start | bytes 245768 | tf_op jit(solution)/shard_map/ppermute | solution.py:375
  16.3 4.4 %collective-permute-start.3 = (bf16[1,4,80,128]{3,2,1,0:T(8,128)(2,1)S(1)}, bf16[1,4,80,128]{3,2,1,0:T(8,128)(2,1)S(1)}, u32[]{:S(2)}, u32[]{:S(2)}) collective-permute-start(bf16[1,4,80,128]{3,2,1,0:T(8,128)(2,1)S(1)} %get-tuple-element.15), channel_id=1, source_target_pairs={{0,2},{1,3},{2,0},{3,1},{4,6},{5,7},{6,4},{7,5},{8,10},{9,11},{10,... | collective-permute-start | bytes 245768 | tf_op jit(solution)/shard_map/ppermute | solution.py:375
  20.8 1.7 %collective-permute-start.6 = (bf16[4,4,80,128]{3,2,1,0:T(8,128)(2,1)S(1)}, bf16[4,4,80,128]{3,2,1,0:T(8,128)(2,1)S(1)}, u32[]{:S(2)}, u32[]{:S(2)}) collective-permute-start(bf16[4,4,80,128]{3,2,1,0:T(8,128)(2,1)S(1)} %get-tuple-element.14), channel_id=1, source_target_pairs={{0,1},{1,0},{2,3},{3,2},{4,5},{5,4},{6,7},{7,6},{8,9},{9,8},{10,11... | collective-permute-start | bytes 983048 | tf_op jit(solution)/shard_map/ppermute | solution.py:377

commit v4 on v3

--- a/solution.py
+++ b/solution.py
@@ -7,6 +7,7 @@
 from jax.experimental import pallas as pl
 from jax.experimental.pallas import tpu as pltpu
 from jax.sharding import PartitionSpec as P
+
 
 WIN = 10
 DECIM = 10
@@ -56,7 +57,6 @@
     for each in small:
         each.start()
     total = x_ref.shape[1]
-    width = groups * 2 * half
     chunk = factor * LANES
     tiles = factor + 1
     tap_count = taps_ref.shape[1]
@@ -278,21 +278,24 @@
             out_ref[group, k * 2 * height : (k + 1) * 2 * height, :] = jnp.where(inside, got, 0.0).astype(BF16)
 
 
-def correlate_kernel(dims, left_ref, parts_ref, out_hbm, *refs):
-    windows, rows, zs, blocks, half, per_group, pack = dims
-    *spec_refs, out_ref, sems = refs
+def correlate_kernel(dims, first_tile, left_ref, parts_ref, *refs):
+    windows, rows, zs, half, per_group, pack, tiles = dims
+    out_hbm, *spec_refs, out_ref, sems = refs if first_tile == 0 else refs[1:]
     height = rows * zs
     depth = 2 * windows
+    per_tile = LANES // height
     block = lax.axis_index("chan")
     own = lax.axis_index("freq")
-    per_tile = LANES // height
+    own_tile, place = block // per_tile, lax.rem(block, per_tile)
     for pair in range(0, windows, 2):
         for tile, spec_ref in enumerate(spec_refs):
             slabs = ([], [])
-            for b in range(tile * per_tile, (tile + 1) * per_tile):
+            for b in range(per_tile):
+                far = place ^ b
                 for z in range(zs):
                     slot = lax.rem(own + zs - z, zs)
-                    got = parts_ref[(block ^ b) & 1, (block ^ b) >> 1, slot, pair * rows : (pair + 2) * rows, :].astype(F32)
+                    at = (far & 1, tile * (per_tile // 2) + (far >> 1), slot, slice(pair * rows, (pair + 2) * rows))
+                    got = parts_ref[at].astype(F32)
                     slabs[0].append(got[:rows])
                     slabs[1].append(got[rows:])
             for e in range(2):
@@ -307,9 +310,15 @@
         prod = jnp.dot(left_ref[group, :, : pack * depth], right, preferred_element_type=F32)
         prod = prod * F32(1.0 / windows)
         first = group * pack
-        out_ref[first : first + pack] = prod.reshape(pack, 2, height, prod.shape[1])
-        copies.append(pltpu.make_async_copy(out_ref.at[pl.ds(first, pack)], out_hbm.at[pl.ds(first, pack)], sems.at[group]))
-        copies[-1].start()
+        for tile in range(tiles):
+            out_ref[tile, first : first + pack] = prod[:, tile * LANES : (tile + 1) * LANES].reshape(pack, 2, height, LANES)
+            columns = pl.ds(pl.multiple_of((own_tile ^ (first_tile + tile)) * LANES, LANES), LANES)
+            copies.append(pltpu.make_async_copy(
+                out_ref.at[tile, pl.ds(first, pack)],
+                out_hbm.at[pl.ds(first, pack), :, :, columns],
+                sems.at[group, tile],
+            ))
+            copies[-1].start()
     for each in copies:
         each.wait()
 
@@ -337,27 +346,30 @@
     )(parts)
 
 
-def correlate(left, parts, per_group, rows):
+def correlate(left, parts, width, first_tile, per_group, rows, so_far=None):
     _, chips, zs, full_rows, lanes = parts.shape
-    blocks = 2 * chips
     windows = full_rows // rows
     half = lanes // 2
     height = rows * zs
-    width = height * blocks
+    tiles = chips * 2 * height // LANES
     pack = pack_of(per_group, windows)
-    dims = (windows, rows, zs, blocks, half, per_group, pack)
+    dims = (windows, rows, zs, half, per_group, pack, tiles)
     vmem = pl.BlockSpec(memory_space=pltpu.VMEM)
-    shape = (per_group, 2, height, width)
+    hbm = pl.BlockSpec(memory_space=pltpu.HBM)
+    given = [] if so_far is None else [so_far]
+    written = per_group * 2 * height * tiles * LANES
     return pl.pallas_call(
-        functools.partial(correlate_kernel, dims),
-        out_shape=jax.ShapeDtypeStruct(shape, F32),
-        in_specs=[vmem, vmem],
-        out_specs=pl.BlockSpec(memory_space=pltpu.HBM),
-        scratch_shapes=[pltpu.VMEM((half * 2 * windows, LANES), F32)] * (width // LANES)
-        + [pltpu.VMEM(shape, F32), pltpu.SemaphoreType.DMA((per_group // pack,))],
-        compiler_params=pltpu.CompilerParams(vmem_limit_bytes=(24 if blocks <= 8 else 44) << 20),
+        functools.partial(correlate_kernel, dims, first_tile),
+        out_shape=jax.ShapeDtypeStruct((per_group, 2, height, width), F32),
+        in_specs=[vmem, vmem] + [hbm] * len(given),
+        out_specs=hbm,
+        input_output_aliases={2: 0} if given else {},
+        scratch_shapes=[pltpu.VMEM((half * 2 * windows, LANES), F32)] * tiles
+        + [pltpu.VMEM((tiles, per_group, 2, height, LANES), F32), pltpu.SemaphoreType.DMA((per_group // pack, tiles))],
+        compiler_params=pltpu.CompilerParams(vmem_limit_bytes=(12 if tiles <= 2 else 44) << 20),
+        cost_estimate=pl.CostEstimate(flops=written * 4 * windows, bytes_accessed=written * 4, transcendentals=0),
         name="correlate",
-    )(left, parts)
+    )(left, parts, *given)
 
 
 def shards(groups, blocks, raw_strain, fir_taps, band_bins, live_mask):
@@ -368,19 +380,32 @@
     for slot in range(1, groups):
         pairs = [(i, (i + slot) % groups) for i in range(groups)]
         got.append(lax.ppermute(pieces[slot], "freq", pairs))
-    parts = jnp.stack(got)
-    left = row_side(parts, per_group, rows)
-    same = [parts[None]]
-    for step in range(2, blocks, 2):
-        same.append(lax.ppermute(parts[None], "chan", [(i, i ^ step) for i in range(blocks)]))
-    same = jnp.concatenate(same, axis=0)
-    other = lax.ppermute(same, "chan", [(i, i ^ 1) for i in range(blocks)])
-    both = jnp.stack([same, other])
-    return correlate(left, both, per_group, rows)
+    parts = jnp.stack(got)[None]
+    left = row_side(parts[0], per_group, rows)
+
+    def swap(array, step):
+        return lax.ppermute(array, "chan", [(i, i ^ step) for i in range(blocks)])
+
+    shared = LANES // (rows * groups) // 2
+    chips = [parts] + [swap(parts, step) for step in range(2, blocks, 2)]
+    near = jnp.concatenate(chips[:shared], axis=0)
+    near, left = lax.optimization_barrier((near, left))
+    near = jnp.stack([near, swap(near, 1)])
+    width = blocks * rows * groups
+    far = jnp.concatenate(chips[shared:], axis=0) if len(chips) > shared else None
+    if far is not None:
+        far, near = lax.optimization_barrier((far, near))
+        far = jnp.stack([far, swap(far, 1)])
+    out = correlate(left, near, width, 0, per_group, rows)
+    if far is not None:
+        out = correlate(left, far, width, 1, per_group, rows, out)
+    return out
 
 
 def solution(mesh):
     in_specs = (P("chan", "freq", None), P(), P(), P("chan", "freq"))
     out_specs = P("freq", None, "chan", None)
-    body = functools.partial(shards, mesh.shape["freq"], mesh.shape["chan"])
+    blocks = mesh.shape["chan"]
+    body = functools.partial(shards, mesh.shape["freq"], blocks)
+
     return jax.shard_map(body, mesh=mesh, in_specs=in_specs, out_specs=out_specs, check_vma=False)

time: 25.2 us -> 24.9 us (0.988)
  waiting for transfers between devices: 7.42 us -> 6.04 us
  Pallas kernels: 6.81 us -> 7.8 us
    ppermute x4 -> x5, waiting for transfers between devices: 4.99 us -> 3.61 us  [swap(): return lax.ppermute(array, 'chan', [(i, i ^ step) for i in range(blocks)])]
    pallas_call x1 -> x2, Pallas kernels: 2.46 us -> 3.47 us  [correlate(): pl.pallas_call(functools.partial(correlate_kernel, dims, first_tile), out...]
    ppermute x4 -> x5, starting transfers between devices: 3.62 us -> 3.7 us  [swap(): return lax.ppermute(array, 'chan', [(i, i ^ step) for i in range(blocks)])]
  transfers between devices with their start and end apart: 7 -> 8, of which waited for: 6 -> 5; matrix products, arithmetic and copies ran while one was open for 0% -> 0% of each run, Pallas kernels for 2% -> 9%
where the time goes in v4:
time: 24.9 us; the launch traced here: 24.8 us
  starting transfers between devices  10.7 us (43%)
  Pallas kernels  7.8 us (31%)
  waiting for transfers between devices  6.04 us (24%)
    ppermute x3, starting transfers between devices, shards(): got.append(lax.ppermute(pieces[slot], 'freq', pairs))  7.04 us
    pallas_call x1, Pallas kernels, front(): pl.pallas_call(functools.partial(front_kernel, dims), out_shape=[jax.Shap...  3.82 us
    ppermute x5, starting transfers between devices, swap(): return lax.ppermute(array, 'chan', [(i, i ^ step) for i in range(blocks)])  3.7 us
    ppermute x5, waiting for transfers between devices, swap(): return lax.ppermute(array, 'chan', [(i, i ^ step) for i in range(blocks)])  3.61 us
    pallas_call x2, Pallas kernels, correlate(): pl.pallas_call(functools.partial(correlate_kernel, dims, first_tile), out...  3.47 us
    ppermute x3, waiting for transfers between devices, shards(): got.append(lax.ppermute(pieces[slot], 'freq', pairs))  2.43 us
    pallas_call x1, Pallas kernels, row_side(): pl.pallas_call(functools.partial(rows_kernel, (windows, rows, zs, half, p...  0.51 us
  transfers between devices with their start and end apart: 8, of which 5 were waited for; matrix products, arithmetic and copies ran while one was open for 0% of the time, Pallas kernels for 9%

profile of v4, /device:TPU:0, one launch (start us, length us, event | category | flops | bytes accessed | tf_op | source)
XLA Modules:
  0.0 24.8 jit_solution(16739826735193023590)
XLA Ops:
  0.0 3.8 %front.1 = (bf16[80,128]{1,0:T(8,128)(2,1)S(1)}, bf16[80,128]{1,0:T(8,128)(2,1)S(1)}, bf16[80,128]{1,0:T(8,128)(2,1)S(1)}, bf16[80,128]{1,0:T(8,128)(2,1)S(1)}) custom-call(s32[1,8]{1,0:T(1,128)} %mask_hbm.1, bf16[1,8,150000]{2,1,0:T(8,128)(2,1)} %x_hbm.1, bf16[1,20]{1,0:T(2,128)(2,1)} %bitcast.21, s32[1,240]{1,0:T(1,128)} %bitcast.20), custom_call_target="tpu_custom_call" | custom-call | tf_op jit(solution)/shard_map/front/pallas_call | solution.py:227
  3.8 3.1 %collective-permute-start = (bf16[80,128]{1,0:T(8,128)(2,1)S(1)}, bf16[80,128]{1,0:T(8,128)(2,1)S(1)}, u32[]{:S(2)}, u32[]{:S(2)}) collective-permute-start(bf16[80,128]{1,0:T(8,128)(2,1)S(1)} %get-tuple-element.14), channel_id=1, source_target_pairs={{0,8},{8,16},{16,24},{24,0},{1,9},{9,17},{17,25},{25,1},{2,10},{10... | collective-permute-start | bytes 61448 | tf_op jit(solution)/shard_map/ppermute | solution.py:382
  6.9 2.6 %collective-permute-start.1 = (bf16[80,128]{1,0:T(8,128)(2,1)S(1)}, bf16[80,128]{1,0:T(8,128)(2,1)S(1)}, u32[]{:S(2)}, u32[]{:S(2)}) collective-permute-start(bf16[80,128]{1,0:T(8,128)(2,1)S(1)} %get-tuple-element.15), channel_id=1, source_target_pairs={{0,16},{8,24},{16,0},{24,8},{1,17},{9,25},{17,1},{25,9},{2,18},{10... | collective-permute-start | bytes 61448 | tf_op jit(solution)/shard_map/ppermute | solution.py:382
  9.5 1.3 %collective-permute-start.2 = (bf16[80,128]{1,0:T(8,128)(2,1)S(1)}, bf16[80,128]{1,0:T(8,128)(2,1)S(1)}, u32[]{:S(2)}, u32[]{:S(2)}) collective-permute-start(bf16[80,128]{1,0:T(8,128)(2,1)S(1)} %get-tuple-element.16), channel_id=1, source_target_pairs={{0,24},{8,0},{16,8},{24,16},{1,25},{9,1},{17,9},{25,17},{2,26},{10... | collective-permute-start | bytes 61448 | tf_op jit(solution)/shard_map/ppermute | solution.py:382
  10.9 0.0 collective-permute-done
  10.9 0.9 %collective-permute-done.1 = bf16[80,128]{1,0:T(8,128)(2,1)S(1)} collective-permute-done((bf16[80,128]{1,0:T(8,128)(2,1)S(1)}, bf16[80,128]{1,0:T(8,128)(2,1)S(1)}, u32[]{:S(2)}, u32[]{:S(2)}) %collective-permute-start.1) | collective-permute-done | bytes 20512 | tf_op jit(solution)/shard_map/ppermute | solution.py:382
  11.8 1.6 %collective-permute-done.2 = bf16[80,128]{1,0:T(8,128)(2,1)S(1)} collective-permute-done((bf16[80,128]{1,0:T(8,128)(2,1)S(1)}, bf16[80,128]{1,0:T(8,128)(2,1)S(1)}, u32[]{:S(2)}, u32[]{:S(2)}) %collective-permute-start.2) | collective-permute-done | bytes 20512 | tf_op jit(solution)/shard_map/ppermute | solution.py:382
  13.3 1.6 %collective-permute-start.3 = (bf16[1,4,80,128]{3,2,1,0:T(8,128)(2,1)S(1)}, bf16[1,4,80,128]{3,2,1,0:T(8,128)(2,1)S(1)}, u32[]{:S(2)}, u32[]{:S(2)}) collective-permute-start(bf16[1,4,80,128]{3,2,1,0:T(8,128)(2,1)S(1)} %get-tuple-element.22), channel_id=1, source_target_pairs={{0,2},{1,3},{2,0},{3,1},{4,6},{5,7},{6,4},{7,5},{8,10},{9,11},{10,... | collective-permute-start | bytes 245768 | tf_op jit(solution)/shard_map/ppermute | solution.py:387
  14.9 1.5 %collective-permute-start.5 = (bf16[1,4,80,128]{3,2,1,0:T(8,128)(2,1)S(1)}, bf16[1,4,80,128]{3,2,1,0:T(8,128)(2,1)S(1)}, u32[]{:S(2)}, u32[]{:S(2)}) collective-permute-start(bf16[1,4,80,128]{3,2,1,0:T(8,128)(2,1)S(1)} %get-tuple-element.22), channel_id=1, source_target_pairs={{0,6},{1,7},{2,4},{3,5},{4,2},{5,3},{6,0},{7,1},{8,14},{9,15},{10,... | collective-permute-start | bytes 245768 | tf_op jit(solution)/shard_map/ppermute | solution.py:387
  16.4 0.5 %collective-permute-start.4 = (bf16[1,4,80,128]{3,2,1,0:T(8,128)(2,1)S(1)}, bf16[1,4,80,128]{3,2,1,0:T(8,128)(2,1)S(1)}, u32[]{:S(2)}, u32[]{:S(2)}) collective-permute-start(bf16[1,4,80,128]{3,2,1,0:T(8,128)(2,1)S(1)} %get-tuple-element.22), channel_id=1, source_target_pairs={{0,4},{1,5},{2,6},{3,7},{4,0},{5,1},{6,2},{7,3},{8,12},{9,13},{10,... | collective-permute-start | bytes 245768 | tf_op jit(solution)/shard_map/ppermute | solution.py:387
  16.9 0.5 %rows.1.left_ref = bf16[15,256,128]{2,1,0:T(8,128)(2,1)S(1)} custom-call(bf16[4,80,128]{2,1,0:T(8,128)(2,1)S(1)} %get-tuple-element.21.parts_ref), custom_call_target="tpu_custom_call" | custom-call | flops 16777216 | bytes 4194304 | tf_op jit(solution)/shard_map/rows/pallas_call | solution.py:337
  17.4 1.0 %collective-permute-done.3 = bf16[1,4,80,128]{3,2,1,0:T(8,128)(2,1)S(1)} collective-permute-done((bf16[1,4,80,128]{3,2,1,0:T(8,128)(2,1)S(1)}, bf16[1,4,80,128]{3,2,1,0:T(8,128)(2,1)S(1)}, u32[]{:S(2)}, u32[]{:S(2)}) %collective-permute-start.3) | collective-permute-done | bytes 81952 | tf_op jit(solution)/shard_map/ppermute | solution.py:387
  18.4 0.1 collective-permute-start.6
  18.5 1.8 %collective-permute-done.5 = bf16[1,4,80,128]{3,2,1,0:T(8,128)(2,1)S(1)} collective-permute-done((bf16[1,4,80,128]{3,2,1,0:T(8,128)(2,1)S(1)}, bf16[1,4,80,128]{3,2,1,0:T(8,128)(2,1)S(1)}, u32[]{:S(2)}, u32[]{:S(2)}) %collective-permute-start.5) | collective-permute-done | bytes 81952 | tf_op jit(solution)/shard_map/ppermute | solution.py:387
  20.2 0.8 %collective-permute-done.4 = bf16[1,4,80,128]{3,2,1,0:T(8,128)(2,1)S(1)} collective-permute-done((bf16[1,4,80,128]{3,2,1,0:T(8,128)(2,1)S(1)}, bf16[1,4,80,128]{3,2,1,0:T(8,128)(2,1)S(1)}, u32[]{:S(2)}, u32[]{:S(2)}) %collective-permute-start.4) | collective-permute-done | bytes 81952 | tf_op jit(solution)/shard_map/ppermute | solution.py:387
  21.1 0.0 collective-permute-done.6
  21.2 0.1 collective-permute-start.7
  21.3 1.7 %correlate.2.refs_0_ = f32[60,2,32,256]{3,2,1,0:T(8,128)} custom-call(bf16[15,256,128]{2,1,0:T(8,128)(2,1)S(1)} %rows.1.left_ref, bf16[2,2,4,80,128]{4,3,2,1,0:T(8,128)(2,1)S(1)} %pad_maximum_fusion.parts_ref), custom_call_target="tpu_custom_call" | custom-call | flops 19660800 | bytes 1966080 | tf_op jit(solution)/shard_map/correlate/pallas_call | solution.py:361
  23.0 0.0 collective-permute-done.7
  23.0 1.7 %correlate.3 = f32[60,2,32,256]{3,2,1,0:T(8,128)} custom-call(bf16[15,256,128]{2,1,0:T(8,128)(2,1)S(1)} %rows.1.left_ref, bf16[2,2,4,80,128]{4,3,2,1,0:T(8,128)(2,1)S(1)} %pad_maximum_fusion.1.parts_ref, f32[60,2,32,256]{3,2,1,0:T(8,128)} %correlate.2.refs_0_), custom_call_target="tpu_custom_call", output_to_operand_aliasing={{}: (2, {})} | custom-call | flops 19660800 | bytes 1966080 | tf_op jit(solution)/shard_map/correlate/pallas_call | solution.py:361
  (5 shorter events, 0.1 us)
Async XLA Ops:
  3.8 7.0 %collective-permute-start = (bf16[80,128]{1,0:T(8,128)(2,1)S(1)}, bf16[80,128]{1,0:T(8,128)(2,1)S(1)}, u32[]{:S(2)}, u32[]{:S(2)}) collective-permute-start(bf16[80,128]{1,0:T(8,128)(2,1)S(1)} %get-tuple-element.14), channel_id=1, source_target_pairs={{0,8},{8,16},{16,24},{24,0},{1,9},{9,17},{17,25},{25,1},{2,10},{10... | collective-permute-start | bytes 61448 | tf_op jit(solution)/shard_map/ppermute | solution.py:382
  6.9 4.8 %collective-permute-start.1 = (bf16[80,128]{1,0:T(8,128)(2,1)S(1)}, bf16[80,128]{1,0:T(8,128)(2,1)S(1)}, u32[]{:S(2)}, u32[]{:S(2)}) collective-permute-start(bf16[80,128]{1,0:T(8,128)(2,1)S(1)} %get-tuple-element.15), channel_id=1, source_target_pairs={{0,16},{8,24},{16,0},{24,8},{1,17},{9,25},{17,1},{25,9},{2,18},{10... | collective-permute-start | bytes 61448 | tf_op jit(solution)/shard_map/ppermute | solution.py:382
  9.5 3.8 %collective-permute-start.2 = (bf16[80,128]{1,0:T(8,128)(2,1)S(1)}, bf16[80,128]{1,0:T(8,128)(2,1)S(1)}, u32[]{:S(2)}, u32[]{:S(2)}) collective-permute-start(bf16[80,128]{1,0:T(8,128)(2,1)S(1)} %get-tuple-element.16), channel_id=1, source_target_pairs={{0,24},{8,0},{16,8},{24,16},{1,25},{9,1},{17,9},{25,17},{2,26},{10... | collective-permute-start | bytes 61448 | tf_op jit(solution)/shard_map/ppermute | solution.py:382
  13.3 5.0 %collective-permute-start.3 = (bf16[1,4,80,128]{3,2,1,0:T(8,128)(2,1)S(1)}, bf16[1,4,80,128]{3,2,1,0:T(8,128)(2,1)S(1)}, u32[]{:S(2)}, u32[]{:S(2)}) collective-permute-start(bf16[1,4,80,128]{3,2,1,0:T(8,128)(2,1)S(1)} %get-tuple-element.22), channel_id=1, source_target_pairs={{0,2},{1,3},{2,0},{3,1},{4,6},{5,7},{6,4},{7,5},{8,10},{9,11},{10,... | collective-permute-start | bytes 245768 | tf_op jit(solution)/shard_map/ppermute | solution.py:387
  14.9 5.4 %collective-permute-start.5 = (bf16[1,4,80,128]{3,2,1,0:T(8,128)(2,1)S(1)}, bf16[1,4,80,128]{3,2,1,0:T(8,128)(2,1)S(1)}, u32[]{:S(2)}, u32[]{:S(2)}) collective-permute-start(bf16[1,4,80,128]{3,2,1,0:T(8,128)(2,1)S(1)} %get-tuple-element.22), channel_id=1, source_target_pairs={{0,6},{1,7},{2,4},{3,5},{4,2},{5,3},{6,0},{7,1},{8,14},{9,15},{10,... | collective-permute-start | bytes 245768 | tf_op jit(solution)/shard_map/ppermute | solution.py:387
  16.4 4.7 %collective-permute-start.4 = (bf16[1,4,80,128]{3,2,1,0:T(8,128)(2,1)S(1)}, bf16[1,4,80,128]{3,2,1,0:T(8,128)(2,1)S(1)}, u32[]{:S(2)}, u32[]{:S(2)}) collective-permute-start(bf16[1,4,80,128]{3,2,1,0:T(8,128)(2,1)S(1)} %get-tuple-element.22), channel_id=1, source_target_pairs={{0,4},{1,5},{2,6},{3,7},{4,0},{5,1},{6,2},{7,3},{8,12},{9,13},{10,... | collective-permute-start | bytes 245768 | tf_op jit(solution)/shard_map/ppermute | solution.py:387
  18.4 2.7 %collective-permute-start.6 = (bf16[2,4,80,128]{3,2,1,0:T(8,128)(2,1)S(1)}, bf16[2,4,80,128]{3,2,1,0:T(8,128)(2,1)S(1)}, u32[]{:S(2)}, u32[]{:S(2)}) collective-permute-start(bf16[2,4,80,128]{3,2,1,0:T(8,128)(2,1)S(1)} %pad_maximum_fusion.2), channel_id=1, source_target_pairs={{0,1},{1,0},{2,3},{3,2},{4,5},{5,4},{6,7},{7,6},{8,9},{9,8},{10,11... | collective-permute-start | bytes 491528 | tf_op jit(solution)/shard_map/ppermute | solution.py:387
  21.2 1.8 %collective-permute-start.7 = (bf16[2,4,80,128]{3,2,1,0:T(8,128)(2,1)S(1)}, bf16[2,4,80,128]{3,2,1,0:T(8,128)(2,1)S(1)}, u32[]{:S(2)}, u32[]{:S(2)}) collective-permute-start(bf16[2,4,80,128]{3,2,1,0:T(8,128)(2,1)S(1)} %pad_maximum_fusion.3), channel_id=1, source_target_pairs={{0,1},{1,0},{2,3},{3,2},{4,5},{5,4},{6,7},{7,6},{8,9},{9,8},{10,11... | collective-permute-start | bytes 491528 | tf_op jit(solution)/shard_map/ppermute | solution.py:387

commit v5 on v4

--- a/solution.py
+++ b/solution.py
@@ -269,13 +269,15 @@
             flipped = jnp.concatenate([straight, swapped, blank], axis=0).T
             for part in range(2):
                 turned_ref[pl.ds(2 * (pair + e) + part, half, stride=depth), :] = flipped[part * half : (part + 1) * half]
-    lane = iota((2 * height, LANES), 1)
-    for group in range(per_group // pack):
-        got = turned_ref[group * pack * depth : (group + 1) * pack * depth, :]
-        got = jnp.concatenate([got, jnp.zeros((LANES - pack * depth, LANES), F32)], axis=0).T[: 2 * height]
-        for k in range(pack):
-            inside = (lane >= k * depth) & (lane < (k + 1) * depth)
-            out_ref[group, k * 2 * height : (k + 1) * 2 * height, :] = jnp.where(inside, got, 0.0).astype(BF16)
+    both = 2 * pack * depth
+    for first in range(0, per_group // pack, 2):
+        at = first * pack * depth
+        size = min(both, turned_ref.shape[0] - at)
+        got = turned_ref[at : at + size, :]
+        got = jnp.concatenate([got, jnp.zeros((LANES - size, LANES), F32)], axis=0).T[: 2 * height]
+        out_ref[first] = got.astype(BF16)
+        if first + 1 < per_group // pack:
+            out_ref[first + 1] = pltpu.roll(got, LANES - pack * depth, 1).astype(BF16)
 
 
 def correlate_kernel(dims, first_tile, left_ref, parts_ref, *refs):
@@ -303,28 +305,31 @@
                 for part in range(2):
                     spec_ref[pl.ds(2 * (pair + e) + part, half, stride=depth), :] = flipped[part * half : (part + 1) * half]
     copies = []
+    row = iota((pack * depth, LANES), 0)
+    burst = 2 if per_group // pack % 2 == 0 else 1
     for group in range(per_group // pack):
         at = group * pack * depth
-        right = [ref[at : at + pack * depth, :] for ref in spec_refs]
-        right = jnp.concatenate(right, axis=1).astype(BF16)
-        prod = jnp.dot(left_ref[group, :, : pack * depth], right, preferred_element_type=F32)
-        prod = prod * F32(1.0 / windows)
-        first = group * pack
         for tile in range(tiles):
-            out_ref[tile, first : first + pack] = prod[:, tile * LANES : (tile + 1) * LANES].reshape(pack, 2, height, LANES)
-            columns = pl.ds(pl.multiple_of((own_tile ^ (first_tile + tile)) * LANES, LANES), LANES)
-            copies.append(pltpu.make_async_copy(
-                out_ref.at[tile, pl.ds(first, pack)],
-                out_hbm.at[pl.ds(first, pack), :, :, columns],
-                sems.at[group, tile],
-            ))
-            copies[-1].start()
+            got = spec_refs[tile][at : at + pack * depth, :]
+            right = [jnp.where((row >= k * depth) & (row < (k + 1) * depth), got, 0.0) for k in range(pack)]
+            right = jnp.concatenate(right, axis=1).astype(BF16)
+            prod = jnp.dot(left_ref[group, :, : pack * depth], right, preferred_element_type=F32)
+            prod = prod * F32(1.0 / windows)
+            for k in range(pack):
+                out_ref[tile, group * pack + k] = prod[:, k * LANES : (k + 1) * LANES].reshape(2, height, LANES)
+            if group % burst == burst - 1:
+                span = pl.ds((group - burst + 1) * pack, burst * pack)
+                columns = pl.ds(pl.multiple_of((own_tile ^ (first_tile + tile)) * LANES, LANES), LANES)
+                copies.append(pltpu.make_async_copy(
+                    out_ref.at[tile, span], out_hbm.at[span, :, :, columns], sems.at[group, tile]
+                ))
+                copies[-1].start()
     for each in copies:
         each.wait()
 
 
 def pack_of(per_group, windows):
-    return next(p for p in (4, 2, 1) if per_group % p == 0 and 2 * windows * p <= LANES)
+    return next(p for p in (2, 1) if per_group % p == 0 and 4 * windows * p <= LANES)
 
 
 def row_side(parts, per_group, rows):
@@ -336,7 +341,7 @@
     vmem = pl.BlockSpec(memory_space=pltpu.VMEM)
     return pl.pallas_call(
         functools.partial(rows_kernel, (windows, rows, zs, half, per_group, pack)),
-        out_shape=jax.ShapeDtypeStruct((per_group // pack, pack * 2 * height, LANES), BF16),
+        out_shape=jax.ShapeDtypeStruct((per_group // pack, 2 * height, LANES), BF16),
         in_specs=[vmem],
         out_specs=vmem,
         scratch_shapes=[pltpu.VMEM((half * 2 * windows, LANES), F32)],

time: 24.9 us -> 25.2 us (1.012)
  Pallas kernels: 7.8 us -> 8.09 us
    pallas_call x2, Pallas kernels: 3.47 us -> 3.73 us  [correlate(): pl.pallas_call(functools.partial(correlate_kernel, dims, first_tile), out...]
  transfers between devices with their start and end apart: 8 -> 8, of which waited for: 5 -> 5; matrix products, arithmetic and copies ran while one was open for 0% -> 0% of each run, Pallas kernels for 9% -> 10%
where the time goes in v5:
time: 25.2 us; the launch traced here: 25 us
  starting transfers between devices  10.7 us (42%)
  Pallas kernels  8.09 us (32%)
  waiting for transfers between devices  6.02 us (24%)
    ppermute x3, starting transfers between devices, shards(): got.append(lax.ppermute(pieces[slot], 'freq', pairs))  7.04 us
    pallas_call x1, Pallas kernels, front(): pl.pallas_call(functools.partial(front_kernel, dims), out_shape=[jax.Shap...  3.82 us
    pallas_call x2, Pallas kernels, correlate(): pl.pallas_call(functools.partial(correlate_kernel, dims, first_tile), out...  3.73 us
    ppermute x5, starting transfers between devices, swap(): return lax.ppermute(array, 'chan', [(i, i ^ step) for i in range(blocks)])  3.7 us
    ppermute x5, waiting for transfers between devices, swap(): return lax.ppermute(array, 'chan', [(i, i ^ step) for i in range(blocks)])  3.58 us
    ppermute x3, waiting for transfers between devices, shards(): got.append(lax.ppermute(pieces[slot], 'freq', pairs))  2.43 us
    pallas_call x1, Pallas kernels, row_side(): pl.pallas_call(functools.partial(rows_kernel, (windows, rows, zs, half, p...  0.54 us
  transfers between devices with their start and end apart: 8, of which 5 were waited for; matrix products, arithmetic and copies ran while one was open for 0% of the time, Pallas kernels for 10%

profile of v5, /device:TPU:0, one launch (start us, length us, event | category | flops | bytes accessed | tf_op | source)
XLA Modules:
  0.0 25.0 jit_solution(6573015943649398187)
XLA Ops:
  0.0 3.8 %front.1 = (bf16[80,128]{1,0:T(8,128)(2,1)S(1)}, bf16[80,128]{1,0:T(8,128)(2,1)S(1)}, bf16[80,128]{1,0:T(8,128)(2,1)S(1)}, bf16[80,128]{1,0:T(8,128)(2,1)S(1)}) custom-call(s32[1,8]{1,0:T(1,128)} %mask_hbm.1, bf16[1,8,150000]{2,1,0:T(8,128)(2,1)} %x_hbm.1, bf16[1,20]{1,0:T(2,128)(2,1)} %bitcast.21, s32[1,240]{1,0:T(1,128)} %bitcast.20), custom_call_target="tpu_custom_call" | custom-call | tf_op jit(solution)/shard_map/front/pallas_call | solution.py:227
  3.8 3.1 %collective-permute-start = (bf16[80,128]{1,0:T(8,128)(2,1)S(1)}, bf16[80,128]{1,0:T(8,128)(2,1)S(1)}, u32[]{:S(2)}, u32[]{:S(2)}) collective-permute-start(bf16[80,128]{1,0:T(8,128)(2,1)S(1)} %get-tuple-element.14), channel_id=1, source_target_pairs={{0,8},{8,16},{16,24},{24,0},{1,9},{9,17},{17,25},{25,1},{2,10},{10... | collective-permute-start | bytes 61448 | tf_op jit(solution)/shard_map/ppermute | solution.py:387
  6.9 2.6 %collective-permute-start.1 = (bf16[80,128]{1,0:T(8,128)(2,1)S(1)}, bf16[80,128]{1,0:T(8,128)(2,1)S(1)}, u32[]{:S(2)}, u32[]{:S(2)}) collective-permute-start(bf16[80,128]{1,0:T(8,128)(2,1)S(1)} %get-tuple-element.15), channel_id=1, source_target_pairs={{0,16},{8,24},{16,0},{24,8},{1,17},{9,25},{17,1},{25,9},{2,18},{10... | collective-permute-start | bytes 61448 | tf_op jit(solution)/shard_map/ppermute | solution.py:387
  9.5 1.3 %collective-permute-start.2 = (bf16[80,128]{1,0:T(8,128)(2,1)S(1)}, bf16[80,128]{1,0:T(8,128)(2,1)S(1)}, u32[]{:S(2)}, u32[]{:S(2)}) collective-permute-start(bf16[80,128]{1,0:T(8,128)(2,1)S(1)} %get-tuple-element.16), channel_id=1, source_target_pairs={{0,24},{8,0},{16,8},{24,16},{1,25},{9,1},{17,9},{25,17},{2,26},{10... | collective-permute-start | bytes 61448 | tf_op jit(solution)/shard_map/ppermute | solution.py:387
  10.9 0.0 collective-permute-done
  10.9 0.9 %collective-permute-done.1 = bf16[80,128]{1,0:T(8,128)(2,1)S(1)} collective-permute-done((bf16[80,128]{1,0:T(8,128)(2,1)S(1)}, bf16[80,128]{1,0:T(8,128)(2,1)S(1)}, u32[]{:S(2)}, u32[]{:S(2)}) %collective-permute-start.1) | collective-permute-done | bytes 20512 | tf_op jit(solution)/shard_map/ppermute | solution.py:387
  11.8 1.6 %collective-permute-done.2 = bf16[80,128]{1,0:T(8,128)(2,1)S(1)} collective-permute-done((bf16[80,128]{1,0:T(8,128)(2,1)S(1)}, bf16[80,128]{1,0:T(8,128)(2,1)S(1)}, u32[]{:S(2)}, u32[]{:S(2)}) %collective-permute-start.2) | collective-permute-done | bytes 20512 | tf_op jit(solution)/shard_map/ppermute | solution.py:387
  13.3 1.6 %collective-permute-start.3 = (bf16[1,4,80,128]{3,2,1,0:T(8,128)(2,1)S(1)}, bf16[1,4,80,128]{3,2,1,0:T(8,128)(2,1)S(1)}, u32[]{:S(2)}, u32[]{:S(2)}) collective-permute-start(bf16[1,4,80,128]{3,2,1,0:T(8,128)(2,1)S(1)} %get-tuple-element.22), channel_id=1, source_target_pairs={{0,2},{1,3},{2,0},{3,1},{4,6},{5,7},{6,4},{7,5},{8,10},{9,11},{10,... | collective-permute-start | bytes 245768 | tf_op jit(solution)/shard_map/ppermute | solution.py:392
  14.9 1.5 %collective-permute-start.5 = (bf16[1,4,80,128]{3,2,1,0:T(8,128)(2,1)S(1)}, bf16[1,4,80,128]{3,2,1,0:T(8,128)(2,1)S(1)}, u32[]{:S(2)}, u32[]{:S(2)}) collective-permute-start(bf16[1,4,80,128]{3,2,1,0:T(8,128)(2,1)S(1)} %get-tuple-element.22), channel_id=1, source_target_pairs={{0,6},{1,7},{2,4},{3,5},{4,2},{5,3},{6,0},{7,1},{8,14},{9,15},{10,... | collective-permute-start | bytes 245768 | tf_op jit(solution)/shard_map/ppermute | solution.py:392
  16.4 0.5 %collective-permute-start.4 = (bf16[1,4,80,128]{3,2,1,0:T(8,128)(2,1)S(1)}, bf16[1,4,80,128]{3,2,1,0:T(8,128)(2,1)S(1)}, u32[]{:S(2)}, u32[]{:S(2)}) collective-permute-start(bf16[1,4,80,128]{3,2,1,0:T(8,128)(2,1)S(1)} %get-tuple-element.22), channel_id=1, source_target_pairs={{0,4},{1,5},{2,6},{3,7},{4,0},{5,1},{6,2},{7,3},{8,12},{9,13},{10,... | collective-permute-start | bytes 245768 | tf_op jit(solution)/shard_map/ppermute | solution.py:392
  16.9 0.5 %rows.1.left_ref = bf16[30,64,128]{2,1,0:T(8,128)(2,1)S(1)} custom-call(bf16[4,80,128]{2,1,0:T(8,128)(2,1)S(1)} %get-tuple-element.21.parts_ref), custom_call_target="tpu_custom_call" | custom-call | flops 16777216 | bytes 4194304 | tf_op jit(solution)/shard_map/rows/pallas_call | solution.py:342
  17.4 0.9 %collective-permute-done.3 = bf16[1,4,80,128]{3,2,1,0:T(8,128)(2,1)S(1)} collective-permute-done((bf16[1,4,80,128]{3,2,1,0:T(8,128)(2,1)S(1)}, bf16[1,4,80,128]{3,2,1,0:T(8,128)(2,1)S(1)}, u32[]{:S(2)}, u32[]{:S(2)}) %collective-permute-start.3) | collective-permute-done | bytes 81952 | tf_op jit(solution)/shard_map/ppermute | solution.py:392
  18.4 0.1 collective-permute-start.6
  18.5 1.8 %collective-permute-done.5 = bf16[1,4,80,128]{3,2,1,0:T(8,128)(2,1)S(1)} collective-permute-done((bf16[1,4,80,128]{3,2,1,0:T(8,128)(2,1)S(1)}, bf16[1,4,80,128]{3,2,1,0:T(8,128)(2,1)S(1)}, u32[]{:S(2)}, u32[]{:S(2)}) %collective-permute-start.5) | collective-permute-done | bytes 81952 | tf_op jit(solution)/shard_map/ppermute | solution.py:392
  20.2 0.8 %collective-permute-done.4 = bf16[1,4,80,128]{3,2,1,0:T(8,128)(2,1)S(1)} collective-permute-done((bf16[1,4,80,128]{3,2,1,0:T(8,128)(2,1)S(1)}, bf16[1,4,80,128]{3,2,1,0:T(8,128)(2,1)S(1)}, u32[]{:S(2)}, u32[]{:S(2)}) %collective-permute-start.4) | collective-permute-done | bytes 81952 | tf_op jit(solution)/shard_map/ppermute | solution.py:392
  21.1 0.0 collective-permute-done.6
  21.2 0.1 collective-permute-start.7
  21.3 1.9 %correlate.2.refs_0_ = f32[60,2,32,256]{3,2,1,0:T(8,128)} custom-call(bf16[30,64,128]{2,1,0:T(8,128)(2,1)S(1)} %rows.1.left_ref, bf16[2,2,4,80,128]{4,3,2,1,0:T(8,128)(2,1)S(1)} %pad_maximum_fusion.parts_ref), custom_call_target="tpu_custom_call" | custom-call | flops 19660800 | bytes 1966080 | tf_op jit(solution)/shard_map/correlate/pallas_call | solution.py:366
  23.1 0.0 collective-permute-done.7
  23.2 1.9 %correlate.3 = f32[60,2,32,256]{3,2,1,0:T(8,128)} custom-call(bf16[30,64,128]{2,1,0:T(8,128)(2,1)S(1)} %rows.1.left_ref, bf16[2,2,4,80,128]{4,3,2,1,0:T(8,128)(2,1)S(1)} %pad_maximum_fusion.1.parts_ref, f32[60,2,32,256]{3,2,1,0:T(8,128)} %correlate.2.refs_0_), custom_call_target="tpu_custom_call", output_to_operand_aliasing={{}: (2, {})} | custom-call | flops 19660800 | bytes 1966080 | tf_op jit(solution)/shard_map/correlate/pallas_call | solution.py:366
  (5 shorter events, 0.1 us)
Async XLA Ops:
  3.8 7.0 %collective-permute-start = (bf16[80,128]{1,0:T(8,128)(2,1)S(1)}, bf16[80,128]{1,0:T(8,128)(2,1)S(1)}, u32[]{:S(2)}, u32[]{:S(2)}) collective-permute-start(bf16[80,128]{1,0:T(8,128)(2,1)S(1)} %get-tuple-element.14), channel_id=1, source_target_pairs={{0,8},{8,16},{16,24},{24,0},{1,9},{9,17},{17,25},{25,1},{2,10},{10... | collective-permute-start | bytes 61448 | tf_op jit(solution)/shard_map/ppermute | solution.py:387
  6.9 4.8 %collective-permute-start.1 = (bf16[80,128]{1,0:T(8,128)(2,1)S(1)}, bf16[80,128]{1,0:T(8,128)(2,1)S(1)}, u32[]{:S(2)}, u32[]{:S(2)}) collective-permute-start(bf16[80,128]{1,0:T(8,128)(2,1)S(1)} %get-tuple-element.15), channel_id=1, source_target_pairs={{0,16},{8,24},{16,0},{24,8},{1,17},{9,25},{17,1},{25,9},{2,18},{10... | collective-permute-start | bytes 61448 | tf_op jit(solution)/shard_map/ppermute | solution.py:387
  9.5 3.8 %collective-permute-start.2 = (bf16[80,128]{1,0:T(8,128)(2,1)S(1)}, bf16[80,128]{1,0:T(8,128)(2,1)S(1)}, u32[]{:S(2)}, u32[]{:S(2)}) collective-permute-start(bf16[80,128]{1,0:T(8,128)(2,1)S(1)} %get-tuple-element.16), channel_id=1, source_target_pairs={{0,24},{8,0},{16,8},{24,16},{1,25},{9,1},{17,9},{25,17},{2,26},{10... | collective-permute-start | bytes 61448 | tf_op jit(solution)/shard_map/ppermute | solution.py:387
  13.3 5.0 %collective-permute-start.3 = (bf16[1,4,80,128]{3,2,1,0:T(8,128)(2,1)S(1)}, bf16[1,4,80,128]{3,2,1,0:T(8,128)(2,1)S(1)}, u32[]{:S(2)}, u32[]{:S(2)}) collective-permute-start(bf16[1,4,80,128]{3,2,1,0:T(8,128)(2,1)S(1)} %get-tuple-element.22), channel_id=1, source_target_pairs={{0,2},{1,3},{2,0},{3,1},{4,6},{5,7},{6,4},{7,5},{8,10},{9,11},{10,... | collective-permute-start | bytes 245768 | tf_op jit(solution)/shard_map/ppermute | solution.py:392
  14.9 5.4 %collective-permute-start.5 = (bf16[1,4,80,128]{3,2,1,0:T(8,128)(2,1)S(1)}, bf16[1,4,80,128]{3,2,1,0:T(8,128)(2,1)S(1)}, u32[]{:S(2)}, u32[]{:S(2)}) collective-permute-start(bf16[1,4,80,128]{3,2,1,0:T(8,128)(2,1)S(1)} %get-tuple-element.22), channel_id=1, source_target_pairs={{0,6},{1,7},{2,4},{3,5},{4,2},{5,3},{6,0},{7,1},{8,14},{9,15},{10,... | collective-permute-start | bytes 245768 | tf_op jit(solution)/shard_map/ppermute | solution.py:392
  16.4 4.7 %collective-permute-start.4 = (bf16[1,4,80,128]{3,2,1,0:T(8,128)(2,1)S(1)}, bf16[1,4,80,128]{3,2,1,0:T(8,128)(2,1)S(1)}, u32[]{:S(2)}, u32[]{:S(2)}) collective-permute-start(bf16[1,4,80,128]{3,2,1,0:T(8,128)(2,1)S(1)} %get-tuple-element.22), channel_id=1, source_target_pairs={{0,4},{1,5},{2,6},{3,7},{4,0},{5,1},{6,2},{7,3},{8,12},{9,13},{10,... | collective-permute-start | bytes 245768 | tf_op jit(solution)/shard_map/ppermute | solution.py:392
  18.4 2.7 %collective-permute-start.6 = (bf16[2,4,80,128]{3,2,1,0:T(8,128)(2,1)S(1)}, bf16[2,4,80,128]{3,2,1,0:T(8,128)(2,1)S(1)}, u32[]{:S(2)}, u32[]{:S(2)}) collective-permute-start(bf16[2,4,80,128]{3,2,1,0:T(8,128)(2,1)S(1)} %pad_maximum_fusion.2), channel_id=1, source_target_pairs={{0,1},{1,0},{2,3},{3,2},{4,5},{5,4},{6,7},{7,6},{8,9},{9,8},{10,11... | collective-permute-start | bytes 491528 | tf_op jit(solution)/shard_map/ppermute | solution.py:392
  21.2 2.0 %collective-permute-start.7 = (bf16[2,4,80,128]{3,2,1,0:T(8,128)(2,1)S(1)}, bf16[2,4,80,128]{3,2,1,0:T(8,128)(2,1)S(1)}, u32[]{:S(2)}, u32[]{:S(2)}) collective-permute-start(bf16[2,4,80,128]{3,2,1,0:T(8,128)(2,1)S(1)} %pad_maximum_fusion.3), channel_id=1, source_target_pairs={{0,1},{1,0},{2,3},{3,2},{4,5},{5,4},{6,7},{7,6},{8,9},{9,8},{10,11... | collective-permute-start | bytes 491528 | tf_op jit(solution)/shard_map/ppermute | solution.py:392

commit v6 on v3

--- a/solution.py
+++ b/solution.py
@@ -45,32 +45,59 @@
     return c, s
 
 
+def stage_cuts(chunks, stages):
+    parts = [5, 5, 4, 2][-stages:]
+    return [up(chunks * sum(parts[:k]) // sum(parts), 2) for k in range(stages)] + [chunks]
+
+
 def front_kernel(dims, mask_hbm, x_hbm, taps_hbm, bins_hbm, *refs):
     windows, length, factor, groups, per_group, half, rows = dims
     outs = refs[:groups]
-    x_ref, mask_ref, taps_ref, bins_ref, band_ref, table_ref, lhs_ref, dec_ref, sems = refs[groups:]
+    tail_ref, mask_ref, taps_ref, bins_ref, band_ref, table_ref, lhs_ref, dec_ref, carry_ref, rows_ref, sems = refs[groups:]
     small = [
         pltpu.make_async_copy(src, dst, sems.at[n])
         for n, (src, dst) in enumerate(((taps_hbm, taps_ref), (bins_hbm, bins_ref), (mask_hbm, mask_ref)))
     ]
     for each in small:
         each.start()
-    total = x_ref.shape[1]
+    total = x_hbm.shape[2]
     width = groups * 2 * half
     chunk = factor * LANES
-    tiles = factor + 1
     tap_count = taps_ref.shape[1]
+    whole = total // chunk
     chunks = -(-total // chunk)
-    stages = sems.shape[0] - len(small)
-    cuts = [up(chunks * k // stages, 2) for k in range(stages)] + [chunks]
-    loads = []
+    stages = sems.shape[0] - len(small) - 1
+    cuts = stage_cuts(chunks, stages)
+
+    bounds, copied, chunk_at, first_at = [0], [], {}, {}
     for k in range(stages):
-        begin, end = cuts[k] * chunk, min(cuts[k + 1] * chunk, total)
-        span = (0, slice(None), pl.ds(begin, end - begin))
-        loads.append(pltpu.make_async_copy(x_hbm.at[span], x_ref.at[span[1:]], sems.at[len(small) + k]))
-        loads[-1].start()
+        at = bounds[-1]
+        chunk_at.update((q, at + q - cuts[k]) for q in range(cuts[k], cuts[k + 1]))
+        copied.append(slice(at * rows, (at + min(cuts[k + 1], whole) - cuts[k]) * rows))
+        at += cuts[k + 1] - cuts[k]
+        for w in range(1, windows):
+            if cuts[k] <= w * length * factor // chunk < cuts[k + 1]:
+                first_at[w] = at
+                at += 1
+        bounds.append(up(at, 2))
+
+    def fetch(k):
+        for q in range(cuts[k], min(cuts[k + 1], whole)):
+            pltpu.make_async_copy(
+                x_hbm.at[0, :, pl.ds(q * chunk, chunk)],
+                lhs_ref.at[pl.ds(chunk_at[q] * rows, rows), :],
+                sems.at[len(small) + k],
+            ).start()
+
+    rest = pltpu.make_async_copy(
+        x_hbm.at[0, :, pl.ds(whole * chunk, total - whole * chunk)], tail_ref, sems.at[len(small) + stages]
+    )
+    fetch(0)
     for each in small:
         each.wait()
+    for k in range(1, stages):
+        fetch(k)
+    rest.start()
 
     period = math.lcm(SUB, factor)
     middle = LANES // 2
@@ -79,20 +106,20 @@
     lane8 = iota((SUB, LANES), 1)
     seeds = []
     for start in range(0, period, SUB):
-        tap = factor * (lane8 - middle) + (factor - 1 + LANES - start) - iota((SUB, LANES), 0)
+        tap = factor * (lane8 - middle) + (factor - 1 - start) - iota((SUB, LANES), 0)
         tap = jnp.where((tap >= 0) & (tap < tap_count), tap, LANES - 1)
         seeds.append(jnp.take_along_axis(taps, tap, axis=1, mode="promise_in_bounds"))
-    for row in range(0, tiles * LANES, 2 * SUB):
-        pair = []
+    nothing = jnp.zeros((SUB, LANES), F32)
+    for row in range(0, chunk, 2 * SUB):
+        inside, beyond = [], []
         for start in (row, row + SUB):
             moved = start // period * (period // factor)
             block = pltpu.roll(seeds[start % period // SUB], (moved - middle) % LANES, 1)
-            if moved < 2 * SUB:
-                block = jnp.where(lane8 < middle, block, 0.0)
-            elif moved > LANES - 2 * SUB:
-                block = jnp.where(lane8 >= middle, block, 0.0)
-            pair.append(block)
-        band_ref[row : row + 2 * SUB, :] = jnp.concatenate(pair, axis=0).astype(BF16)
+            last = moved > LANES - 2 * SUB
+            inside.append(jnp.where(lane8 >= middle, block, 0.0) if last else block)
+            beyond.append(jnp.where(lane8 < middle, block, 0.0) if last else nothing)
+        band_ref[row : row + 2 * SUB, :LANES] = jnp.concatenate(inside, axis=0).astype(BF16)
+        band_ref[row : row + 2 * SUB, LANES:] = jnp.concatenate(beyond, axis=0).astype(BF16)
 
     own = lax.axis_index("freq")
     bin_count = bins_ref.shape[1]
@@ -137,69 +164,85 @@
 
     todo = [(slot, row) for slot in range(groups) for row in range(0, LANES, 2 * SUB)]
 
-    entries = [(q, 0) for q in range(up(chunks, 2))]
-    for w in range(1, windows):
-        begin = w * length * factor
-        entries.append((begin // chunk, begin))
-    edge = up(chunks, 2) - 1
+    def land(k):
+        landed = lhs_ref.at[copied[k], :]
+        pltpu.make_async_copy(landed, landed, sems.at[len(small) + k]).wait()
+        end = bounds[k] + cuts[k + 1] - cuts[k]
+        if cuts[k + 1] > whole:
+            rest.wait()
+            tail = tail_ref[...].astype(F32)
+            tail = jnp.concatenate([tail, jnp.zeros((rows, chunk - tail.shape[1]), F32)], axis=1)
+            lhs_ref[(end - 1) * rows : end * rows, :] = tail.astype(BF16)
+        for w, at in first_at.items():
+            if not bounds[k] <= at < bounds[k + 1]:
+                continue
+            begin = w * length * factor
+            source, lead = chunk_at[begin // chunk] * rows, begin % chunk
+            whole_row = lhs_ref[source : source + rows, :].astype(F32)
+            kept = jnp.where(iota(whole_row.shape, 1) >= lead, whole_row, 0.0)
+            lhs_ref[at * rows : (at + 1) * rows, :] = kept.astype(BF16)
+            end += 1
+        if end < bounds[k + 1]:
+            lhs_ref[end * rows : bounds[k + 1] * rows, :] = jnp.zeros(((bounds[k + 1] - end) * rows, chunk), BF16)
+
+    def decimate(k):
+        middle_at = bounds[k] + up((bounds[k + 1] - bounds[k]) // 2, 2)
+        for begin, end in ((bounds[k], middle_at), (middle_at, bounds[k + 1])):
+            span = slice(begin * rows, end * rows)
+            got = jnp.dot(lhs_ref[span, :], band_ref[...], preferred_element_type=F32)
+            dec_ref[span, :] = got[:, :LANES]
+            carry_ref[span, :] = got[:, LANES:]
+
     zero_tile = jnp.zeros((rows, LANES), F32)
 
-    def tile_of(entry, tile):
-        q, begin = entry
-        start = q * chunk + (tile - 1) * LANES
-        if start < 0 or start >= total or start + LANES <= begin:
-            return zero_tile
-        stop = min(start + LANES, total)
-        got = x_ref[:, start:stop].astype(F32)
-        if stop - start < LANES:
-            got = jnp.concatenate([got, jnp.zeros((rows, LANES - (stop - start)), F32)], axis=1)
-        if start < begin:
-            got = jnp.where(lane8 >= begin - start, got, 0.0)
+    def dec(q, w=None):
+        at = chunk_at[q] if w is None else first_at[w]
+        got = dec_ref[at * rows : (at + 1) * rows, :]
+        if q and w is None:
+            at = chunk_at[q - 1]
+            got = got + carry_ref[at * rows : (at + 1) * rows, :]
         return got
 
-    if len(entries) % 2:
-        entries.append((chunks + 1, 0))
-    bounds = cuts[:-1] + [len(entries)]
+    def window_rows(w):
+        first, lead = divmod(w * length, LANES)
+        span = -(-(length + lead) // LANES)
+        turned = [dec(first, w if w and lead else None)] + [dec(first + n) for n in range(1, span)]
+        if lead:
+            turned = [pltpu.roll(t, LANES - lead, 1) for t in turned]
+        found = []
+        for block in range(blocks):
+            left = length - block * LANES
+            if left <= 0:
+                found.append(zero_tile)
+                continue
+            low = turned[block]
+            if lead and block + 1 < span:
+                low = jnp.where(lane8 < LANES - lead, low, turned[block + 1])
+            found.append(jnp.where(lane8 < left, low, 0.0) if left < LANES else low)
+        return found
+
+    def window_pair(w):
+        for block, pair in enumerate(zip(window_rows(w), window_rows(w + 1))):
+            rows_ref[w * rows : (w + 2) * rows, block * LANES : (block + 1) * LANES] = (
+                jnp.concatenate(pair, axis=0).astype(BF16)
+            )
+
+    waiting = list(range(0, windows, 2))
+
+    def ready_windows(chunks_done):
+        while waiting and -(-(waiting[0] + 2) * length // LANES) <= chunks_done:
+            window_pair(waiting.pop(0))
+
     share = -(-len(todo) // (stages + 1))
     for slot, row in todo[:share]:
         table_rows(slot, row)
     for k in range(stages):
-        loads[k].wait()
-        for pair in range(bounds[k], bounds[k + 1], 2):
-            for tile in range(tiles):
-                both = [tile_of(entries[pair + e], tile) for e in range(2)]
-                lhs_ref[pair * rows : (pair + 2) * rows, tile * LANES : (tile + 1) * LANES] = (
-                    jnp.concatenate(both, axis=0).astype(BF16)
-                )
-        span = slice(bounds[k] * rows, bounds[k + 1] * rows)
-        dec_ref[span, :] = jnp.dot(lhs_ref[span, 0 : tiles * LANES], band_ref[...], preferred_element_type=F32)
+        land(k)
+        decimate(k)
         for slot, row in todo[(k + 1) * share : (k + 2) * share]:
             table_rows(slot, row)
-
-    def dec(entry):
-        return dec_ref[entry * rows : (entry + 1) * rows, :]
-
-    spectrum = None
-    for block in range(blocks):
-        parts = []
-        for w in range(windows):
-            first, lead = divmod(w * length, LANES)
-            entry = first + block
-            low = dec(edge + w) if (block == 0 and w > 0) else dec(entry)
-            if lead:
-                low = pltpu.roll(low, LANES - lead, 1)
-                if entry + 1 < chunks:
-                    high = pltpu.roll(dec(entry + 1), LANES - lead, 1)
-                    low = jnp.where(lane8 < LANES - lead, low, high)
-            left = length - block * LANES
-            if left < LANES:
-                low = jnp.where(lane8 < left, low, 0.0)
-            parts.append(low)
-        lhs = jnp.concatenate(parts, axis=0).astype(BF16)
-        lhs_ref[0 : windows * rows, block * LANES : (block + 1) * LANES] = lhs
-    spectrum = jnp.dot(
-        lhs_ref[0 : windows * rows, 0 : blocks * LANES], table_ref[...], preferred_element_type=F32
-    )
+        ready_windows(cuts[k + 1])
+    spectrum = jnp.dot(rows_ref[...], table_ref[...], preferred_element_type=F32)
     power = jnp.sum(spectrum * spectrum, axis=1, keepdims=True) / bin_count
     row = iota((windows * rows, 1), 0) & (rows - 1)
     live = jnp.zeros((windows * rows, 1), F32)
@@ -220,9 +263,9 @@
     width = groups * 2 * half
     total = raw_strain.shape[2]
     chunks = -(-total // (DECIM * LANES))
-    entries = up(up(chunks, 2) + WIN - 1, 2)
+    stages = 4
+    entries = chunks + WIN - 1 + 2 * stages
     blocks = up(NT, 2 * LANES)
-    stages = 4
     vmem = pl.BlockSpec(memory_space=pltpu.VMEM)
     return pl.pallas_call(
         functools.partial(front_kernel, dims),
@@ -230,15 +273,17 @@
         in_specs=[pl.BlockSpec(memory_space=pltpu.HBM)] * 4,
         out_specs=[vmem] * groups,
         scratch_shapes=[
-            pltpu.VMEM((rows, total), BF16),
+            pltpu.VMEM((rows, total % (DECIM * LANES)), BF16),
             pltpu.SMEM(live_mask.shape, jnp.int32),
             pltpu.VMEM((1, fir_taps.shape[0]), BF16),
             pltpu.VMEM((1, bins), jnp.int32),
-            pltpu.VMEM(((DECIM + 1) * LANES, LANES), BF16),
+            pltpu.VMEM((DECIM * LANES, 2 * LANES), BF16),
             pltpu.VMEM((blocks, width), BF16),
-            pltpu.VMEM((entries * rows, max((DECIM + 1) * LANES, blocks)), BF16),
-            pltpu.VMEM((entries * rows, LANES), F32),
-            pltpu.SemaphoreType.DMA((3 + stages,)),
+            pltpu.VMEM((up(entries, 2) * rows, DECIM * LANES), BF16),
+            pltpu.VMEM((up(entries, 2) * rows, LANES), F32),
+            pltpu.VMEM((up(entries, 2) * rows, LANES), F32),
+            pltpu.VMEM((WIN * rows, blocks), BF16),
+            pltpu.SemaphoreType.DMA((4 + stages,)),
         ],
         compiler_params=pltpu.CompilerParams(vmem_limit_bytes=20 << 20),
         name="front",

time: 25.2 us -> 25.5 us (1.012)
  no operation moved by 1% of the time
where the time goes in v6:
time: 25.5 us; the launch traced here: 25.3 us
  starting transfers between devices  10.7 us (42%)
  waiting for transfers between devices  7.42 us (29%)
  Pallas kernels  7 us (27%)
    ppermute x3, starting transfers between devices, shards(): got.append(lax.ppermute(pieces[slot], 'freq', pairs))  7.04 us
    pallas_call x1, Pallas kernels, front(): pl.pallas_call(functools.partial(front_kernel, dims), out_shape=[jax.Shap...  4.01 us
    ppermute x3, waiting for transfers between devices, shards(): lax.ppermute(parts[None], 'chan', [(i, i ^ step) for i in range(blocks)])  3.91 us
    ppermute x3, starting transfers between devices, shards(): lax.ppermute(parts[None], 'chan', [(i, i ^ step) for i in range(blocks)])  3.55 us
    pallas_call x1, Pallas kernels, correlate(): pl.pallas_call(functools.partial(correlate_kernel, dims), out_shape=jax.S...  2.46 us
    ppermute x3, waiting for transfers between devices, shards(): got.append(lax.ppermute(pieces[slot], 'freq', pairs))  2.43 us
    ppermute x1, waiting for transfers between devices, shards(): other = lax.ppermute(same, 'chan', [(i, i ^ 1) for i in range(blocks)])  1.08 us
    pallas_call x1, Pallas kernels, row_side(): pl.pallas_call(functools.partial(rows_kernel, (windows, rows, zs, half, p...  0.53 us
  transfers between devices with their start and end apart: 7, of which 6 were waited for; matrix products, arithmetic and copies ran while one was open for 0% of the time, Pallas kernels for 2%

profile of v6, /device:TPU:0, one launch (start us, length us, event | category | flops | bytes accessed | tf_op | source)
XLA Modules:
  0.0 25.3 jit_solution(1911464497047275337)
XLA Ops:
  0.0 4.0 %front.1 = (bf16[80,128]{1,0:T(8,128)(2,1)S(1)}, bf16[80,128]{1,0:T(8,128)(2,1)S(1)}, bf16[80,128]{1,0:T(8,128)(2,1)S(1)}, bf16[80,128]{1,0:T(8,128)(2,1)S(1)}) custom-call(s32[1,8]{1,0:T(1,128)} %mask_hbm.1, bf16[1,8,150000]{2,1,0:T(8,128)(2,1)} %x_hbm.1, bf16[1,20]{1,0:T(2,128)(2,1)} %bitcast.17, s32[1,240]{1,0:T(1,128)} %bitcast.16), custom_call_target="tpu_custom_call" | custom-call | tf_op jit(solution)/shard_map/front/pallas_call | solution.py:270
  4.0 3.1 %collective-permute-start = (bf16[80,128]{1,0:T(8,128)(2,1)S(1)}, bf16[80,128]{1,0:T(8,128)(2,1)S(1)}, u32[]{:S(2)}, u32[]{:S(2)}) collective-permute-start(bf16[80,128]{1,0:T(8,128)(2,1)S(1)} %get-tuple-element.10), channel_id=1, source_target_pairs={{0,8},{8,16},{16,24},{24,0},{1,9},{9,17},{17,25},{25,1},{2,10},{10... | collective-permute-start | bytes 61448 | tf_op jit(solution)/shard_map/ppermute | solution.py:415
  7.1 2.6 %collective-permute-start.1 = (bf16[80,128]{1,0:T(8,128)(2,1)S(1)}, bf16[80,128]{1,0:T(8,128)(2,1)S(1)}, u32[]{:S(2)}, u32[]{:S(2)}) collective-permute-start(bf16[80,128]{1,0:T(8,128)(2,1)S(1)} %get-tuple-element.11), channel_id=1, source_target_pairs={{0,16},{8,24},{16,0},{24,8},{1,17},{9,25},{17,1},{25,9},{2,18},{10... | collective-permute-start | bytes 61448 | tf_op jit(solution)/shard_map/ppermute | solution.py:415
  9.7 1.4 %collective-permute-start.2 = (bf16[80,128]{1,0:T(8,128)(2,1)S(1)}, bf16[80,128]{1,0:T(8,128)(2,1)S(1)}, u32[]{:S(2)}, u32[]{:S(2)}) collective-permute-start(bf16[80,128]{1,0:T(8,128)(2,1)S(1)} %get-tuple-element.12), channel_id=1, source_target_pairs={{0,24},{8,0},{16,8},{24,16},{1,25},{9,1},{17,9},{25,17},{2,26},{10... | collective-permute-start | bytes 61448 | tf_op jit(solution)/shard_map/ppermute | solution.py:415
  11.1 0.0 collective-permute-done
  11.1 0.9 %collective-permute-done.1 = bf16[80,128]{1,0:T(8,128)(2,1)S(1)} collective-permute-done((bf16[80,128]{1,0:T(8,128)(2,1)S(1)}, bf16[80,128]{1,0:T(8,128)(2,1)S(1)}, u32[]{:S(2)}, u32[]{:S(2)}) %collective-permute-start.1) | collective-permute-done | bytes 20512 | tf_op jit(solution)/shard_map/ppermute | solution.py:415
  11.9 1.6 %collective-permute-done.2 = bf16[80,128]{1,0:T(8,128)(2,1)S(1)} collective-permute-done((bf16[80,128]{1,0:T(8,128)(2,1)S(1)}, bf16[80,128]{1,0:T(8,128)(2,1)S(1)}, u32[]{:S(2)}, u32[]{:S(2)}) %collective-permute-start.2) | collective-permute-done | bytes 20512 | tf_op jit(solution)/shard_map/ppermute | solution.py:415
  13.5 2.5 %collective-permute-start.5 = (bf16[1,4,80,128]{3,2,1,0:T(8,128)(2,1)S(1)}, bf16[1,4,80,128]{3,2,1,0:T(8,128)(2,1)S(1)}, u32[]{:S(2)}, u32[]{:S(2)}) collective-permute-start(bf16[1,4,80,128]{3,2,1,0:T(8,128)(2,1)S(1)} %get-tuple-element.15), channel_id=1, source_target_pairs={{0,6},{1,7},{2,4},{3,5},{4,2},{5,3},{6,0},{7,1},{8,14},{9,15},{10,... | collective-permute-start | bytes 245768 | tf_op jit(solution)/shard_map/ppermute | solution.py:420
  16.0 0.5 %collective-permute-start.4 = (bf16[1,4,80,128]{3,2,1,0:T(8,128)(2,1)S(1)}, bf16[1,4,80,128]{3,2,1,0:T(8,128)(2,1)S(1)}, u32[]{:S(2)}, u32[]{:S(2)}) collective-permute-start(bf16[1,4,80,128]{3,2,1,0:T(8,128)(2,1)S(1)} %get-tuple-element.15), channel_id=1, source_target_pairs={{0,4},{1,5},{2,6},{3,7},{4,0},{5,1},{6,2},{7,3},{8,12},{9,13},{10,... | collective-permute-start | bytes 245768 | tf_op jit(solution)/shard_map/ppermute | solution.py:420
  16.5 0.5 %collective-permute-start.3 = (bf16[1,4,80,128]{3,2,1,0:T(8,128)(2,1)S(1)}, bf16[1,4,80,128]{3,2,1,0:T(8,128)(2,1)S(1)}, u32[]{:S(2)}, u32[]{:S(2)}) collective-permute-start(bf16[1,4,80,128]{3,2,1,0:T(8,128)(2,1)S(1)} %get-tuple-element.15), channel_id=1, source_target_pairs={{0,2},{1,3},{2,0},{3,1},{4,6},{5,7},{6,4},{7,5},{8,10},{9,11},{10,... | collective-permute-start | bytes 245768 | tf_op jit(solution)/shard_map/ppermute | solution.py:420
  17.1 2.8 %collective-permute-done.5 = bf16[1,4,80,128]{3,2,1,0:T(8,128)(2,1)S(1)} collective-permute-done((bf16[1,4,80,128]{3,2,1,0:T(8,128)(2,1)S(1)}, bf16[1,4,80,128]{3,2,1,0:T(8,128)(2,1)S(1)}, u32[]{:S(2)}, u32[]{:S(2)}) %collective-permute-start.5) | collective-permute-done | bytes 81952 | tf_op jit(solution)/shard_map/ppermute | solution.py:420
  19.8 0.7 %collective-permute-done.4 = bf16[1,4,80,128]{3,2,1,0:T(8,128)(2,1)S(1)} collective-permute-done((bf16[1,4,80,128]{3,2,1,0:T(8,128)(2,1)S(1)}, bf16[1,4,80,128]{3,2,1,0:T(8,128)(2,1)S(1)}, u32[]{:S(2)}, u32[]{:S(2)}) %collective-permute-start.4) | collective-permute-done | bytes 81952 | tf_op jit(solution)/shard_map/ppermute | solution.py:420
  20.6 0.4 %collective-permute-done.3 = bf16[1,4,80,128]{3,2,1,0:T(8,128)(2,1)S(1)} collective-permute-done((bf16[1,4,80,128]{3,2,1,0:T(8,128)(2,1)S(1)}, bf16[1,4,80,128]{3,2,1,0:T(8,128)(2,1)S(1)}, u32[]{:S(2)}, u32[]{:S(2)}) %collective-permute-start.3) | collective-permute-done | bytes 81952 | tf_op jit(solution)/shard_map/ppermute | solution.py:420
  21.0 0.1 fusion.1
  21.0 0.1 collective-permute-start.6
  21.1 0.5 %rows.1.left_ref = bf16[15,256,128]{2,1,0:T(8,128)(2,1)S(1)} custom-call(bf16[4,80,128]{2,1,0:T(8,128)(2,1)S(1)} %get-tuple-element.16.parts_ref), custom_call_target="tpu_custom_call" | custom-call | flops 16777216 | bytes 4194304 | tf_op jit(solution)/shard_map/rows/pallas_call | solution.py:373
  21.7 1.1 %collective-permute-done.6 = bf16[4,4,80,128]{3,2,1,0:T(8,128)(2,1)S(1)} collective-permute-done((bf16[4,4,80,128]{3,2,1,0:T(8,128)(2,1)S(1)}, bf16[4,4,80,128]{3,2,1,0:T(8,128)(2,1)S(1)}, u32[]{:S(2)}, u32[]{:S(2)}) %collective-permute-start.6) | collective-permute-done | bytes 327712 | tf_op jit(solution)/shard_map/ppermute | solution.py:422
  22.7 0.1 pad_maximum_fusion.parts_ref
  22.8 2.5 %correlate.1 = f32[60,2,32,256]{3,2,1,0:T(8,128)} custom-call(bf16[15,256,128]{2,1,0:T(8,128)(2,1)S(1)} %rows.1.left_ref, bf16[2,4,4,80,128]{4,3,2,1,0:T(8,128)(2,1)S(1)} %pad_maximum_fusion.parts_ref), custom_call_target="tpu_custom_call" | custom-call | tf_op jit(solution)/shard_map/correlate/pallas_call | solution.py:396
  (1 shorter events, 0.0 us)
Async XLA Ops:
  4.0 7.0 %collective-permute-start = (bf16[80,128]{1,0:T(8,128)(2,1)S(1)}, bf16[80,128]{1,0:T(8,128)(2,1)S(1)}, u32[]{:S(2)}, u32[]{:S(2)}) collective-permute-start(bf16[80,128]{1,0:T(8,128)(2,1)S(1)} %get-tuple-element.10), channel_id=1, source_target_pairs={{0,8},{8,16},{16,24},{24,0},{1,9},{9,17},{17,25},{25,1},{2,10},{10... | collective-permute-start | bytes 61448 | tf_op jit(solution)/shard_map/ppermute | solution.py:415
  7.1 4.8 %collective-permute-start.1 = (bf16[80,128]{1,0:T(8,128)(2,1)S(1)}, bf16[80,128]{1,0:T(8,128)(2,1)S(1)}, u32[]{:S(2)}, u32[]{:S(2)}) collective-permute-start(bf16[80,128]{1,0:T(8,128)(2,1)S(1)} %get-tuple-element.11), channel_id=1, source_target_pairs={{0,16},{8,24},{16,0},{24,8},{1,17},{9,25},{17,1},{25,9},{2,18},{10... | collective-permute-start | bytes 61448 | tf_op jit(solution)/shard_map/ppermute | solution.py:415
  9.7 3.8 %collective-permute-start.2 = (bf16[80,128]{1,0:T(8,128)(2,1)S(1)}, bf16[80,128]{1,0:T(8,128)(2,1)S(1)}, u32[]{:S(2)}, u32[]{:S(2)}) collective-permute-start(bf16[80,128]{1,0:T(8,128)(2,1)S(1)} %get-tuple-element.12), channel_id=1, source_target_pairs={{0,24},{8,0},{16,8},{24,16},{1,25},{9,1},{17,9},{25,17},{2,26},{10... | collective-permute-start | bytes 61448 | tf_op jit(solution)/shard_map/ppermute | solution.py:415
  13.5 6.3 %collective-permute-start.5 = (bf16[1,4,80,128]{3,2,1,0:T(8,128)(2,1)S(1)}, bf16[1,4,80,128]{3,2,1,0:T(8,128)(2,1)S(1)}, u32[]{:S(2)}, u32[]{:S(2)}) collective-permute-start(bf16[1,4,80,128]{3,2,1,0:T(8,128)(2,1)S(1)} %get-tuple-element.15), channel_id=1, source_target_pairs={{0,6},{1,7},{2,4},{3,5},{4,2},{5,3},{6,0},{7,1},{8,14},{9,15},{10,... | collective-permute-start | bytes 245768 | tf_op jit(solution)/shard_map/ppermute | solution.py:420
  16.0 4.5 %collective-permute-start.4 = (bf16[1,4,80,128]{3,2,1,0:T(8,128)(2,1)S(1)}, bf16[1,4,80,128]{3,2,1,0:T(8,128)(2,1)S(1)}, u32[]{:S(2)}, u32[]{:S(2)}) collective-permute-start(bf16[1,4,80,128]{3,2,1,0:T(8,128)(2,1)S(1)} %get-tuple-element.15), channel_id=1, source_target_pairs={{0,4},{1,5},{2,6},{3,7},{4,0},{5,1},{6,2},{7,3},{8,12},{9,13},{10,... | collective-permute-start | bytes 245768 | tf_op jit(solution)/shard_map/ppermute | solution.py:420
  16.5 4.4 %collective-permute-start.3 = (bf16[1,4,80,128]{3,2,1,0:T(8,128)(2,1)S(1)}, bf16[1,4,80,128]{3,2,1,0:T(8,128)(2,1)S(1)}, u32[]{:S(2)}, u32[]{:S(2)}) collective-permute-start(bf16[1,4,80,128]{3,2,1,0:T(8,128)(2,1)S(1)} %get-tuple-element.15), channel_id=1, source_target_pairs={{0,2},{1,3},{2,0},{3,1},{4,6},{5,7},{6,4},{7,5},{8,10},{9,11},{10,... | collective-permute-start | bytes 245768 | tf_op jit(solution)/shard_map/ppermute | solution.py:420
  21.0 1.7 %collective-permute-start.6 = (bf16[4,4,80,128]{3,2,1,0:T(8,128)(2,1)S(1)}, bf16[4,4,80,128]{3,2,1,0:T(8,128)(2,1)S(1)}, u32[]{:S(2)}, u32[]{:S(2)}) collective-permute-start(bf16[4,4,80,128]{3,2,1,0:T(8,128)(2,1)S(1)} %get-tuple-element.14), channel_id=1, source_target_pairs={{0,1},{1,0},{2,3},{3,2},{4,5},{5,4},{6,7},{7,6},{8,9},{9,8},{10,11... | collective-permute-start | bytes 983048 | tf_op jit(solution)/shard_map/ppermute | solution.py:422
